TPU v7x, 128 devices: a whole 4x4x4 slice. The times are simulated.
128 devices in a mesh: mem: 4 (over z_lo, core), wide: 32 (over x, z_hi, y).
Axes of the slice: x: 4, y: 4, z: 4 (z_hi: 2, z_lo: 2; z = z_hi * 2 + z_lo), core: 2. Of those that a mesh axis runs over, the one named last changes fastest.
Arguments:
- control: float32 [8, 64, 128, 720], P('mem', 'wide'), may hold values from -6 to 6
- perturb: float32 [8, 3, 64, 128, 720], P('mem', None, None, 'wide'), may hold values from -6 to 6
- obs_count: int32 [128, 720], P('wide'), may hold values from 0 to 3
- obs_kind: int32 [128, 720], P('wide'), may hold values from 0 to 7
- obs_table: float32 [8, 192], replicated, may hold values from 0.25 to 4
- band_filter: float32 [64, 64], replicated, may hold values from -0.9 to 1.2, as said below
- diffusivity: float32 [128, 720], replicated, may hold values from 0.04 to 0.24
Outputs:
- hessian_product: float32 [8, 64, 128, 720], P('mem', 'wide')
Inputs may be any that keep to these rules, and one draw needn't show every extreme that they name: band_filter[i, j] is zero where |i - j| > 4; its diagonal lies between 0.8 and 1.2.
All inputs are finite; a program needn't handle non-finite values.
Results may differ from a plain program's by a relative error of at most 0.00005.
Values sent between devices are 32-bit elements; how exact they have to be, the bound alone decides.
No kernel may reach another device: no remote copies, remote signals or barrier semaphores. Data moves between devices by JAX's collectives and lax.ppermute only.
A program may use at most 64 MiB of HBM per device.

v0:
```python
import jax
import jax.numpy as jnp
from jax import lax
from jax.sharding import PartitionSpec as P

ITERS = 16


def split_up(shard, dim, devices):
    before, after = (shard.shape[:dim], shard.shape[dim + 1 :])
    return jnp.moveaxis(shard.reshape(*before, devices, -1, *after), dim, 0)


def sent_and_summed(shard, axis, dim):
    devices = lax.axis_size(axis)
    pieces = lax.all_to_all(split_up(shard, dim, devices), axis, 0, 0, tiled=True)
    return jnp.sum(pieces, axis=0)


def joined_along(pieces, dim):
    pieces = jnp.moveaxis(pieces, 0, dim)
    dims = pieces.shape
    return pieces.reshape(*dims[:dim], dims[dim] * dims[dim + 1], *dims[dim + 2 :])


def sent_to_all(shard, axis):
    copies = jnp.broadcast_to(shard, (lax.axis_size(axis), *shard.shape))
    return lax.all_to_all(copies, axis, split_axis=0, concat_axis=0, tiled=True)


def gathered_copies(shard, axis, dim):
    return joined_along(sent_to_all(shard, axis), dim)


def edge_coeffs(diffusivity):
    east_edge = 0.5 * (diffusivity + jnp.roll(diffusivity, -1, axis=1))
    north_edge = 0.5 * (diffusivity + jnp.roll(diffusivity, -1, axis=0))
    row_index = lax.broadcasted_iota(jnp.int32, diffusivity.shape, 0)
    north_edge = jnp.where(
        row_index < diffusivity.shape[0] - 1, north_edge, jnp.zeros_like(north_edge)
    )
    return (east_edge, north_edge)


def diffuse(field, east_edge, north_edge):

    def one_step(step_index, field_now):
        flux_east = east_edge * (jnp.roll(field_now, -1, axis=-1) - field_now)
        flux_north = north_edge * (jnp.roll(field_now, -1, axis=-2) - field_now)
        increment_field = (
            flux_east
            - jnp.roll(flux_east, 1, axis=-1)
            + flux_north
            - jnp.roll(flux_north, 1, axis=-2)
        )
        return field_now + increment_field

    return lax.fori_loop(0, ITERS, one_step, field)


def weights_for(cell_count, kind_of_cell, table_levels):
    kind_rows = lax.broadcasted_iota(jnp.int32, (table_levels.shape[0],) + kind_of_cell.shape, 0)
    one_hot = (kind_of_cell[None, :, :] == kind_rows).astype(jnp.float32)
    looked_up = jnp.einsum("kvl,kij->vlij", table_levels, one_hot, precision=lax.Precision.HIGHEST)
    return looked_up * cell_count.astype(jnp.float32)[None, None, :, :]


def local(control, perturb, obs_count, obs_kind, obs_table, band_filter, diffusivity):
    highest_level = lax.Precision.HIGHEST
    levels = perturb.shape[2]
    east_edge, north_edge = edge_coeffs(diffusivity)
    table_levels = obs_table.reshape(obs_table.shape[0], 3, levels)
    smooth = diffuse(control, east_edge, north_edge)
    filtered_field = jnp.einsum(
        "lm,kmij->klij",
        band_filter,
        lax.all_to_all(smooth, "wide", split_axis=2, concat_axis=1, tiled=True),
        precision=highest_level,
    )
    partial_accumulated_sum = jnp.einsum(
        "kvlij,klij->vlij", perturb, filtered_field, precision=highest_level
    )
    shared_sum = sent_and_summed(partial_accumulated_sum, "mem", 1)
    share_levels = shared_sum.shape[1]
    first_level = lax.axis_index("mem") * share_levels
    table_share = lax.dynamic_slice_in_dim(table_levels, first_level, share_levels, 2)
    weighted_field = weights_for(obs_count, obs_kind, table_share) * shared_sum
    adjoint_field = jnp.einsum(
        "kvlij,vlij->klij",
        perturb,
        gathered_copies(weighted_field, "mem", 1),
        precision=highest_level,
    )
    lifted = jnp.einsum("lm,klij->kmij", band_filter, adjoint_field, precision=highest_level)
    planes = lax.all_to_all(lifted, "wide", split_axis=1, concat_axis=2, tiled=True)
    spread = diffuse(planes, east_edge, north_edge)
    return control + spread


def solution(mesh):
    placed = (
        P("mem", "wide", None, None),
        P("mem", None, None, "wide", None),
        P("wide", None),
        P("wide", None),
        P(),
        P(),
        P(),
    )
    return jax.shard_map(
        local, mesh=mesh, in_specs=placed, out_specs=P("mem", "wide", None, None), check_vma=False
    )
```

profile of v0, /device:TPU:0, one launch (start us, length us, event | category | flops | bytes accessed | tf_op | source)
XLA Modules:
  0.0 239.3 jit_solution(15836698456583860073)
XLA Ops:
  0.0 1.2 copy.57
  2.6 1.4 copy-done.2
  4.0 46.7 %while.20 = (s32[]{:T(128)}, f32[2,2,128,720]{2,3,1,0:T(8,128)S(1)}, f32[128,720]{0,1:T(8,128)S(1)}, f32[128,720]{0,1:T(8,128)S(1)}, s32[]{:T(128)}) while((s32[]{:T(128)}, f32[2,2,128,720]{2,3,1,0:T(8,128)S(1)}, f32[128,720]{0,1:T(8,128)S(1)}, f32[128,720]{0,1:T(8,128)S(1)}, s32[]{:T(128)}) %tuple.51), condition=%wide.region_1.2_spmd, body=%wide.region_0.1_spmd.sunk | while | flops 4423682 | bytes 22859836 | solution.py:58
  4.6 0.6 fusion.34
  5.6 1.3 fusion.35
  8.6 1.3 fusion.35
  11.5 1.3 fusion.35
  14.4 1.3 fusion.35
  16.3 0.6 fusion.34
  17.3 1.3 fusion.35
  19.2 0.6 fusion.34
  20.2 1.3 fusion.35
  22.1 0.6 fusion.34
  23.2 1.3 fusion.35
  25.0 0.6 fusion.34
  26.1 1.3 fusion.35
  27.9 0.6 fusion.34
  29.0 1.3 fusion.35
  30.9 0.6 fusion.34
  31.9 1.3 fusion.35
  33.8 0.6 fusion.34
  34.8 1.3 fusion.35
  36.7 0.6 fusion.34
  37.8 1.3 fusion.35
  39.6 0.6 fusion.34
  40.7 1.3 fusion.35
  43.6 1.3 fusion.35
  46.5 1.3 fusion.35
  49.5 1.3 fusion.35
  50.8 1.0 copy.63
  51.8 35.1 %all_to_all.46 = f32[2,2,128,720]{3,1,0,2:T(2,128)S(1)} all-to-all(f32[2,2,128,720]{3,1,0,2:T(2,128)S(1)} %copy.63), channel_id=1, replica_groups=mesh['mem'=4,'wide'=32] {'wide'}, dimensions={2} | all-to-all | bytes 2949120 | tf_op jit(solution)/shard_map/all_to_all | solution.py:77
  87.3 1.7 fusion.15
  89.0 1.0 copy.96
  90.0 4.6 %multiply_reduce_fusion.1 = f32[64,4,720,3]{2,1,0,3:T(4,128)S(1)} fusion(f32[2,3,64,4,720]{4,3,2,1,0:T(4,128)} %param.12, f32[64,4,720,2]{2,1,0,3:T(4,128)S(1)} %copy.96), kind=kLoop, calls=%fused_computation.17 | loop fusion | flops 1658880 | bytes 8110080
  95.0 1.6 copy.67
  96.7 3.8 %all-to-all-start.1 = ((f32[4,3,16,4,720]{4,2,3,1,0:T(8,128)}), f32[4,3,16,4,720]{4,2,3,1,0:T(8,128)S(1)}, u32[]{:S(2)}, u32[]{:S(2)}) async-start(f32[4,3,16,4,720]{4,2,3,1,0:T(8,128)} %copy.67), calls=%async_computation.1 | async-start | bytes 4718592 | tf_op jit(solution)/shard_map/all_to_all | solution.py:16
  100.6 28.2 %all-to-all-done.1 = f32[4,3,16,4,720]{4,2,3,1,0:T(8,128)S(1)} async-done(((f32[4,3,16,4,720]{4,2,3,1,0:T(8,128)}), f32[4,3,16,4,720]{4,2,3,1,0:T(8,128)S(1)}, u32[]{:S(2)}, u32[]{:S(2)}) %all-to-all-start.1) | async-done | bytes 2211872 | tf_op jit(solution)/shard_map/all_to_all | solution.py:16
  129.9 31.2 %all_to_all.47 = f32[4,3,16,4,720]{4,2,3,1,0:T(8,128)S(1)} all-to-all(f32[4,3,16,4,720]{4,2,3,1,0:T(8,128)S(1)} %broadcast_in_dim.7), channel_id=1, replica_groups=mesh['mem'=4,'wide'=32] {'mem'}, dimensions={0} | all-to-all | bytes 4423680 | tf_op jit(solution)/shard_map/all_to_all | solution.py:28
  161.2 1.5 copy.97
  162.8 1.8 multiply_reduce_fusion
  164.6 1.7 fusion.18
  166.3 1.0 copy.70
  167.3 27.7 %all_to_all.48 = f32[2,64,4,720]{3,2,0,1:T(4,128)S(1)} all-to-all(f32[2,64,4,720]{3,2,0,1:T(4,128)S(1)} %copy.70), channel_id=1, replica_groups=mesh['mem'=4,'wide'=32] {'wide'}, dimensions={1} | all-to-all | bytes 2949120 | tf_op jit(solution)/shard_map/all_to_all | solution.py:95
  195.1 0.8 copy.71
  196.0 0.8 copy-done.4
  196.9 38.2 %while.21 = (s32[]{:T(128)}, f32[2,2,128,720]{3,2,1,0:T(8,128)S(1)}, f32[128,720]{1,0:T(8,128)S(1)}, f32[128,720]{1,0:T(8,128)S(1)}, s32[]{:T(128)}) while((s32[]{:T(128)}, f32[2,2,128,720]{3,2,1,0:T(8,128)S(1)}, f32[128,720]{1,0:T(8,128)S(1)}, f32[128,720]{1,0:T(8,128)S(1)}, s32[]{:T(128)}) %tuple.52), condition=%wide.region_4.5_spmd, body=%wide.region_3.4_spmd.sunk | while | flops 4423682 | bytes 22882876 | solution.py:58
  198.1 1.1 fusion.37
  200.5 1.1 fusion.37
  202.9 1.1 fusion.37
  205.3 1.1 fusion.37
  207.6 1.1 fusion.37
  210.0 1.1 fusion.37
  212.4 1.1 fusion.37
  214.8 1.1 fusion.37
  217.2 1.1 fusion.37
  219.6 1.1 fusion.37
  222.0 1.1 fusion.37
  224.4 1.1 fusion.37
  226.7 1.1 fusion.37
  229.1 1.1 fusion.37
  231.5 1.1 fusion.37
  233.9 1.1 fusion.37
  235.1 1.6 copy.73
  236.7 2.6 %add.33 = f32[2,2,128,720]{2,3,1,0:T(8,128)} add(f32[2,2,128,720]{2,3,1,0:T(8,128)S(1)} %copy-done.1, f32[2,2,128,720]{2,3,1,0:T(8,128)} %copy.73) | non-fusion elementwise | flops 368640 | bytes 4423680 | tf_op jit(solution)/shard_map/add | solution.py:97
  (237 shorter events, 41.8 us)
Async XLA Ops:
  0.0 87.3 %copy-start = (f32[64,64]{1,0:T(8,128)S(1)}, f32[64,64]{1,0:T(8,128)}, u32[]{:S(2)}) copy-start(f32[64,64]{1,0:T(8,128)} %param.16) | copy-start | bytes 49156
  0.0 1.5 slice-start.2
  1.7 0.7 copy-start.3
  2.6 1.4 copy-start.2
  96.7 3.8 %copy-start.7 = (f32[8,192]{1,0:T(8,128)S(1)}, f32[8,192]{1,0:T(8,128)}, u32[]{:S(2)}) copy-start(f32[8,192]{1,0:T(8,128)} %param.15) | copy-start | bytes 18436
  96.7 3.9 %copy-start.6 = (s32[4,720]{1,0:T(4,128)S(1)}, s32[4,720]{1,0:T(4,128)}, u32[]{:S(2)}) copy-start(s32[4,720]{1,0:T(4,128)} %param.13) | copy-start | bytes 34564
  96.7 32.2 %all-to-all-start.1 = ((f32[4,3,16,4,720]{4,2,3,1,0:T(8,128)}), f32[4,3,16,4,720]{4,2,3,1,0:T(8,128)S(1)}, u32[]{:S(2)}, u32[]{:S(2)}) async-start(f32[4,3,16,4,720]{4,2,3,1,0:T(8,128)} %copy.67), calls=%async_computation.1 | async-start | bytes 4718592 | tf_op jit(solution)/shard_map/all_to_all | solution.py:16
  100.4 28.7 %copy-start.5 = (s32[4,720]{1,0:T(4,128)S(1)}, s32[4,720]{1,0:T(4,128)}, u32[]{:S(2)}) copy-start(s32[4,720]{1,0:T(4,128)} %param.14) | copy-start | bytes 34564
  129.9 32.9 %slice-start = ((s8[4718592]{0:T(1024)(128)(4,1)}), s8[4194304]{0:T(1024)(128)(4,1)S(1)}, s32[]{:S(2)}) async-start(s8[4718592]{0:T(1024)(128)(4,1)} %bitcast.69), calls=%async_computation.4 | async-start | bytes 8388608
  161.1 1.7 slice-start.1
  195.9 1.0 copy-start.4
  235.1 1.6 copy-start.1
where the time goes:
time: 240 us; the launch traced here: 239 us
  blocking collectives  94 us (39%)
  other arithmetic  64.4 us (27%)
  local copies, waits for them, and re-layouts  42.9 us (18%)
  waiting for transfers between devices  28.2 us (12%)
  matrix products  3.85 us (2%)
  starting transfers between devices  3.76 us (2%)
    add x32, other arithmetic, one_step(): return field_now + increment_field  38.9 us
    all_to_all x1, blocking collectives, local(): lax.all_to_all(smooth, 'wide', split_axis=2, concat_axis=1, tiled=True)  35.1 us
    all_to_all x1, blocking collectives, sent_to_all(): return lax.all_to_all(copies, axis, split_axis=0, concat_axis=0, tiled=True)  31.2 us
    all_to_all x1, waiting for transfers between devices, sent_and_summed(): lax.all_to_all(split_up(shard, dim, devices), axis, 0, 0, tiled=True)  28.2 us
    all_to_all x1, blocking collectives, local(): lax.all_to_all(lifted, 'wide', split_axis=1, concat_axis=2, tiled=True)  27.7 us
    mul x32, other arithmetic, one_step(): flux_east = east_edge * (jnp.roll(field_now, -1, axis=-1) - field_now)  16.1 us
    slice x64, local copies, waits for them, and re-layouts, one_step(): flux_east = east_edge * (jnp.roll(field_now, -1, axis=-1) - field_now)  9.45 us
    slice x48, local copies, waits for them, and re-layouts, one_step(): flux_north = north_edge * (jnp.roll(field_now, -1, axis=-2) - field_now)  9.29 us
  transfers between devices with their start and end apart: 1, of which 1 were waited for; matrix products, arithmetic and copies ran while one was open for 0% of the time, Pallas kernels for 0%

commit v1 on v0

v1 whole, which is shorter than its diff:
```python
import jax
import jax.numpy as jnp
from jax import lax
from jax.experimental import pallas as pl
from jax.experimental.pallas import tpu as pltpu
from jax.sharding import PartitionSpec as P

ITERS = 16
SUB = 8
VMEM = pl.BlockSpec(memory_space=pltpu.VMEM)
HIGHEST = lax.Precision.HIGHEST


def coefficients(diff_ref, east, north, steps, lanes):
    lane = lax.broadcasted_iota(jnp.int32, (SUB, lanes), 1)
    cells = [diff_ref[pl.ds(r, SUB, stride=steps), :] for r in range(steps)]
    wrapped = pltpu.roll(cells[0], SUB - 1, 0)
    for r in range(steps):
        here = cells[r]
        there = cells[r + 1] if r + 1 < steps else wrapped
        east[r] = 0.5 * (here + there)
        up = 0.5 * (here + pltpu.roll(here, lanes - 1, 1))
        north[r] = jnp.where(lane < lanes - 1, up, jnp.zeros_like(up))


def diffuse_in_place(field, east, north, planes, steps, lanes):
    def one_step(step_index, carry):
        first = [field[q, 0] for q in range(planes)]
        ahead = [pltpu.roll(f, SUB - 1, 0) for f in first]
        here = list(first)
        before = [
            pltpu.roll(east[steps - 1] * (ahead[q] - field[q, steps - 1]), 1, 0)
            for q in range(planes)
        ]
        for r in range(steps):
            east_r, north_r = east[r], north[r]
            for q in range(planes):
                there = field[q, r + 1] if r + 1 < steps else ahead[q]
                flux_east = east_r * (there - here[q])
                flux_north = north_r * (pltpu.roll(here[q], lanes - 1, 1) - here[q])
                change = (flux_east - before[q]) + (flux_north - pltpu.roll(flux_north, 1, 1))
                field[q, r] = here[q] + change
                before[q] = flux_east
                here[q] = there
        return carry

    lax.fori_loop(0, ITERS, one_step, 0)


def spread_out(control_ref, diff_ref, out_ref, east, north, field, plain):
    planes, lon, lat = control_ref.shape
    steps = lon // SUB
    rows = lat // out_ref.shape[0]
    coefficients(diff_ref, east, north, steps, lat)
    for q in range(planes):
        for r in range(steps):
            field[q, r] = control_ref[q, pl.ds(r, SUB, stride=steps), :]
    diffuse_in_place(field, east, north, planes, steps, lat)
    for q in range(planes):
        for r in range(steps):
            plain[q, pl.ds(r, SUB, stride=steps), :] = field[q, r]
        for start in range(0, lon, 128):
            width = min(128, lon - start)
            turned = plain[q, start : start + 128, :].T
            for d in range(lat // rows):
                out_ref[d, rows * q : rows * q + rows, start : start + width] = turned[
                    rows * d : rows * d + rows, :width
                ]


def gather_in(pieces_ref, control_ref, diff_ref, out_ref, east, north, field, plain, whole):
    planes, lon, lat = control_ref.shape
    steps = lon // SUB
    devices = pieces_ref.shape[0]
    rows = lat // devices
    coefficients(diff_ref, east, north, steps, lat)
    for q in range(planes):
        for d in range(devices):
            whole[rows * d : rows * d + rows, :lon] = pieces_ref[d, rows * q : rows * q + rows, :]
        for start in range(0, lon, 128):
            plain[q, start : start + 128, :] = whole[:, start : start + 128].T
        for r in range(steps):
            field[q, r] = plain[q, pl.ds(r, SUB, stride=steps), :]
    diffuse_in_place(field, east, north, planes, steps, lat)
    for q in range(planes):
        for r in range(steps):
            place = pl.ds(r, SUB, stride=steps)
            out_ref[q, place, :] = control_ref[q, place, :] + field[q, r]


def partial_sums(core_ref, band_ref, first_ref, second_ref, perturb_ref, *rest):
    outs, filtered = rest[:6], rest[6]
    rows = first_ref.shape[0]
    half = rows // 2
    filtered[0] = first_ref[...]
    filtered[1] = jnp.dot(
        band_ref[...], second_ref[...], precision=HIGHEST, preferred_element_type=jnp.float32
    )
    core = core_ref[0]
    for side in range(2):
        base = (core if side else 1 - core) * half

        def body(t, carry, side=side, base=base):
            at = pl.ds(pl.multiple_of(base + t * SUB, SUB), SUB)
            to = pl.ds(pl.multiple_of(t * SUB, SUB), SUB)
            f0, f1 = filtered[0, at, :], filtered[1, at, :]
            for v in range(3):
                outs[3 * side + v][to, :] = (
                    perturb_ref[0, v, at, :] * f0 + perturb_ref[1, v, at, :] * f1
                )
            return carry

        lax.fori_loop(0, half // SUB, body, 0)


def lift(core_ref, band_ref, perturb_ref, *rest):
    own, other, out_ref, adjoint = rest[:3], rest[3:6], rest[6], rest[7]
    rows = out_ref.shape[0]
    half = rows // 2
    core = core_ref[0]
    for side in range(2):
        base = (core if side == 0 else 1 - core) * half
        weighted = own if side == 0 else other

        def body(t, carry, base=base, weighted=weighted):
            at = pl.ds(pl.multiple_of(base + t * SUB, SUB), SUB)
            to = pl.ds(pl.multiple_of(t * SUB, SUB), SUB)
            total = perturb_ref[0, at, :] * weighted[0][to, :]
            for v in (1, 2):
                total = total + perturb_ref[v, at, :] * weighted[v][to, :]
            adjoint[at, :] = total
            return carry

        lax.fori_loop(0, half // SUB, body, 0)
    out_ref[...] = jnp.dot(
        band_ref[...], adjoint[...], precision=HIGHEST, preferred_element_type=jnp.float32
    )


def call(kernel, out_shape, scratch, flops, moved, smem_first=False):
    def run(*args):
        specs = [VMEM] * len(args)
        if smem_first:
            specs[0] = pl.BlockSpec(memory_space=pltpu.SMEM)
        return pl.pallas_call(
            kernel,
            out_shape=out_shape,
            in_specs=specs,
            out_specs=jax.tree.map(lambda _: VMEM, out_shape),
            scratch_shapes=scratch,
            cost_estimate=pl.CostEstimate(flops=flops, bytes_accessed=moved, transcendentals=0),
            compiler_params=pltpu.CompilerParams(vmem_limit_bytes=40 << 20),
        )(*args)

    return run


def f32(*shape):
    return jax.ShapeDtypeStruct(shape, jnp.float32)


def local(control, perturb, obs_count, obs_kind, obs_table, band_filter, diffusivity):
    members, planes, lat, lon = control.shape
    kinds = obs_table.shape[0]
    variables, levels, rows = perturb.shape[1:4]
    devices = lax.axis_size("wide")
    steps = lon // SUB
    flat = levels * rows
    half = flat // 2
    padded = -(-lon // 128) * 128
    control_t = jnp.swapaxes(control, 2, 3)
    diff_t = jnp.swapaxes(diffusivity, 0, 1)
    core = lax.axis_index("mem") % 2

    coefs = [pltpu.VMEM((steps, SUB, lat), jnp.float32)] * 2
    field = pltpu.VMEM((planes, steps, SUB, lat), jnp.float32)
    plain = pltpu.VMEM((planes, padded, lat), jnp.float32)
    whole = pltpu.VMEM((lat, padded), jnp.float32)
    work = planes * lat * lon * ITERS * 8
    size = planes * lat * lon * 4

    def to_rows(k):
        sent = call(spread_out, f32(devices, planes * rows, lon), [*coefs, field, plain], work, 2 * size)(
            control_t[k], diff_t
        )
        got = lax.all_to_all(sent, "wide", 0, 0, tiled=True)
        return got.reshape(flat, lon)

    def to_planes(k, lifted):
        got = lax.all_to_all(
            lifted.reshape(devices, planes * rows, lon), "wide", 0, 0, tiled=True
        )
        return call(gather_in, f32(planes, lon, lat), [*coefs, field, plain, whole], work, 3 * size)(
            got, control_t[k], diff_t
        )

    smooth = [to_rows(k) for k in range(members)]

    eye = jnp.eye(rows, dtype=jnp.float32)
    band = (band_filter[:, None, :, None] * eye[None, :, None, :]).reshape(flat, flat)
    band_t = (band_filter.T[:, None, :, None] * eye[None, :, None, :]).reshape(flat, flat)
    perturb_rows = perturb.reshape(members, variables, flat, lon)

    kind_rows = lax.broadcasted_iota(jnp.int32, (kinds,) + obs_kind.shape, 0)
    one_hot = jnp.where(obs_kind[None] == kind_rows, obs_count[None], 0).astype(jnp.float32)
    table = lax.dynamic_slice_in_dim(
        obs_table.reshape(kinds, variables, levels), core * (levels // 2), levels // 2, 2
    )
    weights = jnp.einsum("kvl,kij->vlij", table, one_hot, precision=HIGHEST)
    weights = weights.reshape(variables, half, lon)

    filtered = jnp.dot(band, smooth[0], precision=HIGHEST)
    scalar = core.astype(jnp.int32).reshape(1)
    parts = call(
        partial_sums,
        [f32(half, lon)] * 6,
        [pltpu.VMEM((members, flat, lon), jnp.float32)],
        2 * flat * flat * lon,
        12 * flat * lon * 4,
        True,
    )(scalar, band, filtered, smooth[1], perturb_rows)

    other_core = [(i, i ^ 1) for i in range(4)]
    next_chip = [(i, i ^ 2) for i in range(4)]
    own, other = [], []
    for v in range(variables):
        on_chip = parts[3 + v] + lax.ppermute(parts[v], "mem", other_core)
        total = on_chip + lax.ppermute(on_chip, "mem", next_chip)
        own.append(weights[v] * total)
        other.append(lax.ppermute(own[v], "mem", other_core))

    out = []
    for k in range(members):
        lifted = call(
            lift,
            f32(flat, lon),
            [pltpu.VMEM((flat, lon), jnp.float32)],
            2 * flat * flat * lon,
            8 * flat * lon * 4,
            True,
        )(scalar, band_t, perturb_rows[k], *own, *other)
        out.append(to_planes(k, lifted))
    return jnp.swapaxes(jnp.stack(out), 2, 3)


def solution(mesh):
    placed = (
        P("mem", "wide", None, None),
        P("mem", None, None, "wide", None),
        P("wide", None),
        P("wide", None),
        P(),
        P(),
        P(),
    )
    return jax.shard_map(
        local, mesh=mesh, in_specs=placed, out_specs=P("mem", "wide", None, None), check_vma=False
    )
```

time: 240 us -> 179 us (0.75)
  blocking collectives: 94 us -> 0 us
  Pallas kernels: 0 us -> 47.9 us
  other arithmetic: 64.4 us -> 16.6 us
  starting transfers between devices: 3.76 us -> 33.7 us
  local copies, waits for them, and re-layouts: 42.9 us -> 49.8 us
    all_to_all x3 -> x0, blocking collectives: 94 us -> none  [the longest x1 35.1 us: local(): lax.all_to_all(smooth, 'wide', split_axis=2, concat_axis=1, tiled=True)]
    pallas_call x0 -> x7, Pallas kernels: none -> 47.9 us  [run(): pl.pallas_call(kernel, out_shape=out_shape, in_specs=specs, out_specs=jax...]
    add x33 -> x3, other arithmetic: 41.5 us -> 3.68 us  [local(): on_chip = parts[3 + v] + lax.ppermute(parts[v], 'mem', other_core)]
    all_to_all x1 -> x4, starting transfers between devices: 3.76 us -> 29.8 us  [the longest x2 15.3 us: to_rows(): got = lax.all_to_all(sent, 'wide', 0, 0, tiled=True)]
    slice x182 -> x5, local copies, waits for them, and re-layouts: 28.4 us -> 6.2 us  [the longest x1 5.34 us: local(): perturb_rows[k]]
    mul x0 -> x2, local copies, waits for them, and re-layouts: none -> 17.2 us  [the longest x1 8.91 us: local(): band_filter.T[:, None, :, None] * eye[None, :, None, :]]
    all_to_all x1 -> x4, waiting for transfers between devices: 28.2 us -> 17.4 us  [the longest x2 12.2 us: to_planes(): lax.all_to_all(lifted.reshape(devices, planes * rows, lon), 'wide', 0, 0,...]
    unnamed x23 -> x35, local copies, waits for them, and re-layouts: 6.59 us -> 16.3 us
  transfers between devices with their start and end apart: 1 -> 13, of which waited for: 1 -> 6; matrix products, arithmetic and copies ran while one was open for 0% -> 32% of each run, Pallas kernels for 0% -> 13%
where the time goes in v1:
time: 179 us; the launch traced here: 178 us
  local copies, waits for them, and re-layouts  49.8 us (28%)
  Pallas kernels  47.9 us (27%)
  starting transfers between devices  33.7 us (19%)
  waiting for transfers between devices  26.3 us (15%)
  other arithmetic  16.6 us (9%)
  matrix products  3.07 us (2%)
    pallas_call x7, Pallas kernels, run(): pl.pallas_call(kernel, out_shape=out_shape, in_specs=specs, out_specs=jax...  47.9 us
    unnamed x35, local copies, waits for them, and re-layouts  16.3 us
    all_to_all x2, starting transfers between devices, to_rows(): got = lax.all_to_all(sent, 'wide', 0, 0, tiled=True)  15.3 us
    all_to_all x2, starting transfers between devices, to_planes(): lax.all_to_all(lifted.reshape(devices, planes * rows, lon), 'wide', 0, 0,...  14.5 us
    all_to_all x2, waiting for transfers between devices, to_planes(): lax.all_to_all(lifted.reshape(devices, planes * rows, lon), 'wide', 0, 0,...  12.2 us
    mul x1, local copies, waits for them, and re-layouts, local(): band_filter.T[:, None, :, None] * eye[None, :, None, :]  8.91 us
    mul x1, local copies, waits for them, and re-layouts, local(): band_filter[:, None, :, None] * eye[None, :, None, :]  8.29 us
    ppermute x3, waiting for transfers between devices, local(): total = on_chip + lax.ppermute(on_chip, 'mem', next_chip)  7.86 us
  transfers between devices with their start and end apart: 13, of which 6 were waited for; matrix products, arithmetic and copies ran while one was open for 32% of the time, Pallas kernels for 13%

profile of v1, /device:TPU:0, one launch (start us, length us, event | category | flops | bytes accessed | tf_op | source)
XLA Modules:
  0.0 177.6 jit_solution(14305647476890474885)
XLA Ops:
  0.0 1.5 slice_bitcast_fusion
  1.5 0.0 copy-start.13
  1.5 10.1 %shard_map.73 = f32[32,8,720]{2,1,0:T(8,128)} custom-call(f32[2,720,128]{2,1,0:T(8,128)S(1)} %get-tuple-element.20.control_ref, f32[720,128]{1,0:T(8,128)S(1)} %bitcast.32), custom_call_target="tpu_custom_call" | custom-call | flops 23592960 | bytes 1474560 | tf_op jit(solution)/shard_map/pallas_call | solution.py:145
  11.7 10.7 %all-to-all-start = ((f32[32,8,720]{2,1,0:T(8,128)}), f32[32,8,720]{2,1,0:T(8,128)S(1)}, u32[]{:S(2)}, u32[]{:S(2)}) async-start(f32[32,8,720]{2,1,0:T(8,128)} %shard_map.73), calls=%async_computation | async-start | bytes 1572864 | tf_op jit(solution)/shard_map/all_to_all | solution.py:186
  22.4 0.1 copy.13
  22.5 10.2 %shard_map.74 = f32[32,8,720]{2,1,0:T(8,128)} custom-call(f32[2,720,128]{2,1,0:T(8,128)S(1)} %get-tuple-element.19.control_ref, f32[720,128]{1,0:T(8,128)S(1)} %bitcast.33), custom_call_target="tpu_custom_call" | custom-call | flops 23592960 | bytes 1474560 | tf_op jit(solution)/shard_map/pallas_call | solution.py:145
  32.7 5.2 %all-to-all-done = f32[32,8,720]{2,1,0:T(8,128)S(1)} async-done(((f32[32,8,720]{2,1,0:T(8,128)}), f32[32,8,720]{2,1,0:T(8,128)S(1)}, u32[]{:S(2)}, u32[]{:S(2)}) %all-to-all-start) | async-done | bytes 737312 | tf_op jit(solution)/shard_map/all_to_all | solution.py:186
  37.9 0.9 copy-done.12
  38.8 4.6 %all-to-all-start.1 = ((f32[32,8,720]{2,1,0:T(8,128)}), f32[32,8,720]{2,1,0:T(8,128)S(1)}, u32[]{:S(2)}, u32[]{:S(2)}) async-start(f32[32,8,720]{2,1,0:T(8,128)} %shard_map.74), calls=%async_computation.1 | async-start | bytes 1572864 | tf_op jit(solution)/shard_map/all_to_all | solution.py:186
  43.4 6.9 %broadcast_multiply_fusion = (f32[64,4,64,4]{3,2,1,0:T(8,128)}, f32[64,4,64,4]{3,2,1,0:T(8,128)}) fusion(f32[64,64]{1,0:T(8,128)S(1)} %copy-done.13, f32[4,4]{1,0:T(4,128)S(1)} %fusion.9, f32[64,64]{1,0:T(8,128)S(1)} %copy.13), kind=kLoop, calls=%fused_computation | loop fusion | flops 131072 | bytes 557120 | tf_op jit(solution)/shard_map/mul | solution.py:200
  50.3 8.3 %mul.60.band_ref = f32[256,256]{1,0:T(8,128)S(1)} reshape(f32[64,4,64,4]{3,2,1,0:T(8,128)} %get-tuple-element.24) | data formatting | bytes 524288 | tf_op jit(solution)/shard_map/mul | solution.py:200
  58.5 6.0 %copy.16 = f32[2,3,64,4,720]{4,0,3,2,1:T(2,128)S(1)} copy(f32[2,3,64,4,720]{4,3,2,1,0:T(4,128)} %param.8) | data formatting | bytes 8847360 | tf_op args[1]
  64.5 2.7 %copy.18.perturb_ref = f32[2,3,256,720]{3,2,1,0:T(8,128)} copy(f32[2,3,256,720]{3,0,2,1:T(2,128)S(1)} %bitcast.41) | data formatting | bytes 8847360 | tf_op jit(solution)/shard_map/reshape | solution.py:202
  67.2 2.0 %fusion.first_ref = f32[256,720]{1,0:T(8,128)S(1)} fusion(f32[256,256]{1,0:T(8,128)S(1)} %mul.60.band_ref, f32[32,8,720]{2,1,0:T(8,128)} %copy-done.12), kind=kOutput, calls=%fused_computation.3 | convolution fusion | flops 566231040 | bytes 1736704 | tf_op jit(solution)/shard_map/dot_general | solution.py:212
  69.2 0.0 all-to-all-done.1
  69.2 2.3 %copy-done = f32[2,3,256,720]{3,2,1,0:T(8,128)S(1)} copy-done((f32[2,3,256,720]{3,2,1,0:T(8,128)S(1)}, f32[2,3,256,720]{3,2,1,0:T(8,128)}, u32[]{:S(2)}) %copy-start) | copy-done | bytes 4423704
  71.5 2.2 %shard_map.75 = (f32[128,720]{1,0:T(8,128)}, f32[128,720]{1,0:T(8,128)}, f32[128,720]{1,0:T(8,128)S(1)}, f32[128,720]{1,0:T(8,128)S(1)}, f32[128,720]{1,0:T(8,128)S(1)}, /*index=5*/f32[128,720]{1,0:T(8,128)S(1)}) custom-call(s32[1]{0:T(128)} %bitcast.core_ref, f32[256,256]{1,0:T(8,128)S(1)} %mul.60.band_ref, f32[256,720]{1,0:T(8,128)S(1)} %fusion.first_ref, ...), custom_call_target="tpu_custom_call" | custom-call | flops 94371840 | bytes 8847360 | tf_op jit(solution)/shard_map/pallas_call | solution.py:145
  73.7 0.8 copy-done.8
  74.5 0.8 copy-done.10
  75.3 0.7 copy-done.11
  76.1 0.5 collective-permute-start.2
  76.6 0.1 reshape.63
  76.6 0.1 constant_dynamic-slice_fusion
  76.7 0.2 collective-permute-start.4
  76.9 1.1 collective-permute-done
  78.0 1.8 %add.27 = f32[128,720]{1,0:T(8,128)} add(f32[128,720]{1,0:T(8,128)} %copy-done.10, f32[128,720]{1,0:T(8,128)S(1)} %collective-permute-done) | non-fusion elementwise | flops 92160 | bytes 1105920 | tf_op jit(solution)/shard_map/add | solution.py:227
  79.8 1.0 collective-permute-start.1
  80.8 1.1 fusion.2
  82.0 0.8 add.29
  82.8 1.0 collective-permute-start.3
  83.8 0.1 fusion.12
  83.9 8.9 %mul.56.band_ref = f32[256,256]{1,0:T(8,128)} reshape(f32[64,4,64,4]{3,2,1,0:T(8,128)} %get-tuple-element.25) | data formatting | bytes 524288 | tf_op jit(solution)/shard_map/mul | solution.py:201
  92.8 0.3 copy.15
  93.1 0.1 squeeze.24
  93.2 0.3 copy.19
  93.5 0.1 squeeze.27
  93.6 0.3 copy.20
  93.9 0.1 squeeze.28
  94.0 1.1 add.31
  95.1 1.1 collective-permute-start.5
  96.2 2.0 %add_multiply_fusion.2.rest_0_ = f32[128,720]{1,0:T(8,128)} fusion(f32[128,720]{1,0:T(8,128)S(1)} %squeeze.24, f32[128,720]{1,0:T(8,128)} %add.27, f32[128,720]{1,0:T(8,128)} %collective-permute-done.1), kind=kLoop, calls=%fused_computation.9 | loop fusion | flops 184320 | bytes 1474560 | tf_op jit(solution)/shard_map/mul | solution.py:229
  98.2 2.4 %collective-permute-done.3 = f32[128,720]{1,0:T(8,128)} collective-permute-done((f32[128,720]{1,0:T(8,128)}, f32[128,720]{1,0:T(8,128)}, u32[]{:S(2)}, u32[]{:S(2)}) %collective-permute-start.3) | collective-permute-done | bytes 368672 | tf_op jit(solution)/shard_map/ppermute | solution.py:228
  100.5 2.0 %add_multiply_fusion.1.rest_1_ = f32[128,720]{1,0:T(8,128)} fusion(f32[128,720]{1,0:T(8,128)S(1)} %squeeze.27, f32[128,720]{1,0:T(8,128)} %add.29, f32[128,720]{1,0:T(8,128)} %collective-permute-done.3), kind=kLoop, calls=%fused_computation.8 | loop fusion | flops 184320 | bytes 1474560 | tf_op jit(solution)/shard_map/mul | solution.py:229
  102.5 0.0 collective-permute-start.7
  102.5 5.5 %collective-permute-done.5 = f32[128,720]{1,0:T(8,128)S(1)} collective-permute-done((f32[128,720]{1,0:T(8,128)S(1)}, f32[128,720]{1,0:T(8,128)S(1)}, u32[]{:S(2)}, u32[]{:S(2)}) %collective-permute-start.5) | collective-permute-done | bytes 368672 | tf_op jit(solution)/shard_map/ppermute | solution.py:228
  108.0 0.8 add_multiply_fusion.rest_2_
  108.8 5.3 %fusion.11 = (f32[1,3,64,4,720]{4,3,2,1,0:T(4,128)}, f32[1,3,64,4,720]{4,3,2,1,0:T(4,128)}) fusion(f32[2,3,64,4,720]{4,3,2,1,0:T(4,128)} %param.8), kind=kLoop, calls=%fused_computation.23 | loop fusion | bytes 8847360 | tf_op jit(solution)/shard_map/slice | solution.py:241
  114.2 2.7 %squeeze.29.perturb_ref = f32[3,256,720]{2,1,0:T(8,128)S(1)} reshape(f32[1,3,64,4,720]{4,3,2,1,0:T(4,128)} %get-tuple-element.18) | data formatting | bytes 4423680 | tf_op jit(solution)/shard_map/squeeze | solution.py:241
  116.9 0.9 copy-done.6
  117.8 2.7 %shard_map.78 = f32[256,720]{1,0:T(8,128)S(1)} custom-call(s32[1]{0:T(128)} %bitcast.core_ref, f32[256,256]{1,0:T(8,128)S(1)} %copy-done.6, f32[3,256,720]{2,1,0:T(8,128)S(1)} %squeeze.29.perturb_ref, f32[128,720]{1,0:T(8,128)} %add_multiply_fusion.2.rest_0_, f32[128,720]{1,0:T(8,128)} %add_multiply_fusion.1.rest_1_, f32[128,720]{1,0:T(8,128)} %add_multiply_fusion.rest_2_, ...), custom_call_target="tpu_custom_call" | custom-call | flops 94371840 | bytes 5898240 | tf_op jit(solution)/shard_map/pallas_call | solution.py:145
  120.6 0.0 copy-start.5
  120.6 0.9 copy-done.5
  121.5 9.9 %all-to-all-start.3 = ((f32[32,8,720]{2,1,0:T(8,128)}), f32[32,8,720]{2,1,0:T(8,128)}, u32[]{:S(2)}, u32[]{:S(2)}) async-start(f32[32,8,720]{2,1,0:T(8,128)} %bitcast.38), calls=%async_computation.3 | async-start | bytes 1572864 | tf_op jit(solution)/shard_map/all_to_all | solution.py:190
  131.4 2.7 %squeeze.23.perturb_ref = f32[3,256,720]{2,1,0:T(8,128)S(1)} reshape(f32[1,3,64,4,720]{4,3,2,1,0:T(4,128)} %get-tuple-element.17) | data formatting | bytes 4423680 | tf_op jit(solution)/shard_map/squeeze | solution.py:241
  134.1 0.9 copy-done.7
  135.0 2.7 %shard_map.76 = f32[256,720]{1,0:T(8,128)S(1)} custom-call(s32[1]{0:T(128)} %bitcast.core_ref, f32[256,256]{1,0:T(8,128)S(1)} %copy-done.7, f32[3,256,720]{2,1,0:T(8,128)S(1)} %squeeze.23.perturb_ref, f32[128,720]{1,0:T(8,128)} %add_multiply_fusion.2.rest_0_, f32[128,720]{1,0:T(8,128)} %add_multiply_fusion.1.rest_1_, f32[128,720]{1,0:T(8,128)} %add_multiply_fusion.rest_2_, ...), custom_call_target="tpu_custom_call" | custom-call | flops 94371840 | bytes 5898240 | tf_op jit(solution)/shard_map/pallas_call | solution.py:145
  137.8 0.9 copy-done.4
  138.7 8.5 %all-to-all-done.3.pieces_ref = f32[32,8,720]{2,1,0:T(8,128)} async-done(((f32[32,8,720]{2,1,0:T(8,128)}), f32[32,8,720]{2,1,0:T(8,128)}, u32[]{:S(2)}, u32[]{:S(2)}) %all-to-all-start.3) | async-done | bytes 737312 | tf_op jit(solution)/shard_map/all_to_all | solution.py:190
  147.2 4.6 %all-to-all-start.2 = ((f32[32,8,720]{2,1,0:T(8,128)}), f32[32,8,720]{2,1,0:T(8,128)S(1)}, u32[]{:S(2)}, u32[]{:S(2)}) async-start(f32[32,8,720]{2,1,0:T(8,128)} %bitcast.37), calls=%async_computation.2 | async-start | bytes 1572864 | tf_op jit(solution)/shard_map/all_to_all | solution.py:190
  151.8 1.1 copy-done.2
  152.9 10.5 %shard_map.79 = f32[2,720,128]{2,1,0:T(8,128)S(1)} custom-call(f32[32,8,720]{2,1,0:T(8,128)} %all-to-all-done.3.pieces_ref, f32[2,720,128]{2,1,0:T(8,128)S(1)} %copy-done.2, f32[720,128]{1,0:T(8,128)S(1)} %bitcast.34), custom_call_target="tpu_custom_call" | custom-call | flops 23592960 | bytes 2211840 | tf_op jit(solution)/shard_map/pallas_call | solution.py:145
  163.4 3.6 %all-to-all-done.2.pieces_ref = f32[32,8,720]{2,1,0:T(8,128)S(1)} async-done(((f32[32,8,720]{2,1,0:T(8,128)}), f32[32,8,720]{2,1,0:T(8,128)S(1)}, u32[]{:S(2)}, u32[]{:S(2)}) %all-to-all-start.2) | async-done | bytes 737312 | tf_op jit(solution)/shard_map/all_to_all | solution.py:190
  167.0 9.4 %shard_map.77 = f32[2,720,128]{2,1,0:T(8,128)S(1)} custom-call(f32[32,8,720]{2,1,0:T(8,128)S(1)} %all-to-all-done.2.pieces_ref, f32[2,720,128]{2,1,0:T(8,128)S(1)} %get-tuple-element.20.control_ref, f32[720,128]{1,0:T(8,128)S(1)} %bitcast.35), custom_call_target="tpu_custom_call" | custom-call | flops 23592960 | bytes 2211840 | tf_op jit(solution)/shard_map/pallas_call | solution.py:145
  176.4 1.2 maximum_bitcast_fusion
  (32 shorter events, 0.1 us)
Async XLA Ops:
  0.0 1.5 copy-start.3
  1.5 31.2 %copy-start.1 = (f32[2,720,128]{2,1,0:T(8,128)}, f32[2,720,128]{2,1,0:T(8,128)S(1)}, u32[]{:S(2)}) copy-start(f32[2,720,128]{2,1,0:T(8,128)S(1)} %get-tuple-element.19.control_ref) | copy-start | bytes 2211844
  1.5 20.9 %copy-start.13 = (f32[64,64]{1,0:T(8,128)S(1)}, f32[64,64]{1,0:T(8,128)}, u32[]{:S(2)}) copy-start(f32[64,64]{1,0:T(8,128)} %param.12) | copy-start | bytes 49156
  11.7 26.2 %all-to-all-start = ((f32[32,8,720]{2,1,0:T(8,128)}), f32[32,8,720]{2,1,0:T(8,128)S(1)}, u32[]{:S(2)}, u32[]{:S(2)}) async-start(f32[32,8,720]{2,1,0:T(8,128)} %shard_map.73), calls=%async_computation | async-start | bytes 1572864 | tf_op jit(solution)/shard_map/all_to_all | solution.py:186
  37.9 0.9 copy-start.12
  38.8 30.4 %all-to-all-start.1 = ((f32[32,8,720]{2,1,0:T(8,128)}), f32[32,8,720]{2,1,0:T(8,128)S(1)}, u32[]{:S(2)}, u32[]{:S(2)}) async-start(f32[32,8,720]{2,1,0:T(8,128)} %shard_map.74), calls=%async_computation.1 | async-start | bytes 1572864 | tf_op jit(solution)/shard_map/all_to_all | solution.py:186
  69.2 2.3 %copy-start = (f32[2,3,256,720]{3,2,1,0:T(8,128)S(1)}, f32[2,3,256,720]{3,2,1,0:T(8,128)}, u32[]{:S(2)}) copy-start(f32[2,3,256,720]{3,2,1,0:T(8,128)} %copy.18.perturb_ref) | copy-start | bytes 13271044
  71.5 5.1 %copy-start.16 = (f32[8,192]{1,0:T(8,128)S(1)}, f32[8,192]{1,0:T(8,128)}, u32[]{:S(2)}) copy-start(f32[8,192]{1,0:T(8,128)} %param.11) | copy-start | bytes 18436
  71.5 9.3 %copy-start.14 = (s32[4,720]{1,0:T(4,128)S(1)}, s32[4,720]{1,0:T(4,128)}, u32[]{:S(2)}) copy-start(s32[4,720]{1,0:T(4,128)} %param.9) | copy-start | bytes 34564
  71.5 9.3 %copy-start.15 = (s32[4,720]{1,0:T(4,128)S(1)}, s32[4,720]{1,0:T(4,128)}, u32[]{:S(2)}) copy-start(s32[4,720]{1,0:T(4,128)} %param.10) | copy-start | bytes 34564
  73.7 0.8 copy-start.8
  74.5 0.8 copy-start.10
  75.3 0.8 copy-start.11
  76.1 5.9 %copy-start.9 = (f32[128,720]{1,0:T(8,128)S(1)}, f32[128,720]{1,0:T(8,128)}, u32[]{:S(2)}) copy-start(f32[128,720]{1,0:T(8,128)} %copy-done.8) | copy-start | bytes 1105924
  76.1 1.9 %collective-permute-start = (f32[128,720]{1,0:T(8,128)}, f32[128,720]{1,0:T(8,128)S(1)}, u32[]{:S(2)}, u32[]{:S(2)}) collective-permute-start(f32[128,720]{1,0:T(8,128)} %get-tuple-element.12), channel_id=1, source_target_pairs={{0,32},{32,0},{64,96},{96,64},{1,33},{33,1},{65,97},{97,65},{2,34}... | collective-permute-start | bytes 1105928 | tf_op jit(solution)/shard_map/ppermute | solution.py:227
  76.1 5.9 %collective-permute-start.2 = (f32[128,720]{1,0:T(8,128)}, f32[128,720]{1,0:T(8,128)S(1)}, u32[]{:S(2)}, u32[]{:S(2)}) collective-permute-start(f32[128,720]{1,0:T(8,128)} %get-tuple-element.14), channel_id=1, source_target_pairs={{0,32},{32,0},{64,96},{96,64},{1,33},{33,1},{65,97},{97,65},{2,34}... | collective-permute-start | bytes 1105928 | tf_op jit(solution)/shard_map/ppermute | solution.py:227
  76.7 17.3 %collective-permute-start.4 = (f32[128,720]{1,0:T(8,128)}, f32[128,720]{1,0:T(8,128)}, u32[]{:S(2)}, u32[]{:S(2)}) collective-permute-start(f32[128,720]{1,0:T(8,128)} %copy-done.11), channel_id=1, source_target_pairs={{0,32},{32,0},{64,96},{96,64},{1,33},{33,1},{65,97},{97,65},{2,34}... | collective-permute-start | bytes 1105928 | tf_op jit(solution)/shard_map/ppermute | solution.py:227
  79.8 16.4 %collective-permute-start.1 = (f32[128,720]{1,0:T(8,128)}, f32[128,720]{1,0:T(8,128)}, u32[]{:S(2)}, u32[]{:S(2)}) collective-permute-start(f32[128,720]{1,0:T(8,128)} %add.27), channel_id=1, source_target_pairs={{0,64},{32,96},{64,0},{96,32},{1,65},{33,97},{65,1},{97,33},{2,66}... | collective-permute-start | bytes 1105928 | tf_op jit(solution)/shard_map/ppermute | solution.py:228
  82.8 17.7 %collective-permute-start.3 = (f32[128,720]{1,0:T(8,128)}, f32[128,720]{1,0:T(8,128)}, u32[]{:S(2)}, u32[]{:S(2)}) collective-permute-start(f32[128,720]{1,0:T(8,128)} %add.29), channel_id=1, source_target_pairs={{0,64},{32,96},{64,0},{96,32},{1,65},{33,97},{65,1},{97,33},{2,66}... | collective-permute-start | bytes 1105928 | tf_op jit(solution)/shard_map/ppermute | solution.py:228
  95.1 12.9 %collective-permute-start.5 = (f32[128,720]{1,0:T(8,128)S(1)}, f32[128,720]{1,0:T(8,128)S(1)}, u32[]{:S(2)}, u32[]{:S(2)}) collective-permute-start(f32[128,720]{1,0:T(8,128)S(1)} %add.31), channel_id=1, source_target_pairs={{0,64},{32,96},{64,0},{96,32},{1,65},{33,97},{65,1},{97,33},{2,66}... | collective-permute-start | bytes 1105928 | tf_op jit(solution)/shard_map/ppermute | solution.py:228
  98.2 18.7 %collective-permute-start.6 = (f32[128,720]{1,0:T(8,128)}, f32[128,720]{1,0:T(8,128)}, u32[]{:S(2)}, u32[]{:S(2)}) collective-permute-start(f32[128,720]{1,0:T(8,128)} %add_multiply_fusion.2.rest_0_), channel_id=1, source_target_pairs={{0,32},{32,0},{64,96},{96,64},{1,33},{33,1},{65,97},{97,65},{2,34}... | collective-permute-start | bytes 1105928 | tf_op jit(solution)/shard_map/ppermute | solution.py:230
  102.5 14.4 %collective-permute-start.7 = (f32[128,720]{1,0:T(8,128)}, f32[128,720]{1,0:T(8,128)}, u32[]{:S(2)}, u32[]{:S(2)}) collective-permute-start(f32[128,720]{1,0:T(8,128)} %add_multiply_fusion.1.rest_1_), channel_id=1, source_target_pairs={{0,32},{32,0},{64,96},{96,64},{1,33},{33,1},{65,97},{97,65},{2,34}... | collective-permute-start | bytes 1105928 | tf_op jit(solution)/shard_map/ppermute | solution.py:230
  108.8 8.0 %collective-permute-start.8 = (f32[128,720]{1,0:T(8,128)}, f32[128,720]{1,0:T(8,128)}, u32[]{:S(2)}, u32[]{:S(2)}) collective-permute-start(f32[128,720]{1,0:T(8,128)} %add_multiply_fusion.rest_2_), channel_id=1, source_target_pairs={{0,32},{32,0},{64,96},{96,64},{1,33},{33,1},{65,97},{97,65},{2,34}... | collective-permute-start | bytes 1105928 | tf_op jit(solution)/shard_map/ppermute | solution.py:230
  116.9 1.0 copy-start.6
  120.6 0.9 copy-start.5
  121.5 25.7 %all-to-all-start.3 = ((f32[32,8,720]{2,1,0:T(8,128)}), f32[32,8,720]{2,1,0:T(8,128)}, u32[]{:S(2)}, u32[]{:S(2)}) async-start(f32[32,8,720]{2,1,0:T(8,128)} %bitcast.38), calls=%async_computation.3 | async-start | bytes 1572864 | tf_op jit(solution)/shard_map/all_to_all | solution.py:190
  134.1 1.0 copy-start.7
  137.8 0.9 copy-start.4
  147.2 19.9 %all-to-all-start.2 = ((f32[32,8,720]{2,1,0:T(8,128)}), f32[32,8,720]{2,1,0:T(8,128)S(1)}, u32[]{:S(2)}, u32[]{:S(2)}) async-start(f32[32,8,720]{2,1,0:T(8,128)} %bitcast.37), calls=%async_computation.2 | async-start | bytes 1572864 | tf_op jit(solution)/shard_map/all_to_all | solution.py:190
  151.8 1.1 copy-start.2

commit v2 on v0

v2 whole, which is shorter than its diff:
```python
import jax
import jax.numpy as jnp
from jax import lax
from jax.experimental import pallas as pl
from jax.experimental.pallas import tpu as pltpu
from jax.sharding import PartitionSpec as P

ITERS = 16
SUB = 8
LANES = 128
VMEM = pl.BlockSpec(memory_space=pltpu.VMEM)
SMEM = pl.BlockSpec(memory_space=pltpu.SMEM)
HIGHEST = lax.Precision.HIGHEST


def dot(a, b, contract=((1,), (0,))):
    return lax.dot_general(
        a, b, (contract, ((), ())), precision=HIGHEST, preferred_element_type=jnp.float32
    )


def iota(shape, dim):
    return lax.broadcasted_iota(jnp.int32, shape, dim)


def ones_where(mask):
    return jnp.where(mask, 1.0, 0.0).astype(jnp.float32)


def blocks_of(lon):
    return [(start, min(LANES, lon - start)) for start in range(0, lon, LANES)]


def coefficients(diff_ref, east, north, turned, flat):
    rows, steps = east.shape[:2]
    lon, lat = diff_ref.shape
    blocks = lat // rows
    copies = LANES // blocks
    for start, width in blocks_of(lon):
        turned[start // LANES, :lat, :width] = diff_ref[start : start + width, :].T
    for i in range(rows):
        for start, width in blocks_of(lon):
            picked = turned[start // LANES, pl.ds(i, blocks, stride=rows), :]
            flat[i, start : start + LANES, :] = jnp.concatenate([picked] * copies, 0).T
    edge = lax.rem(iota((SUB, LANES), 1), blocks) == blocks - 1
    first = [flat[i, pl.ds(0, SUB, stride=steps), :] for i in range(rows)]
    here = list(first)
    for r in range(steps):
        for i in range(rows):
            if r + 1 < steps:
                there = flat[i, pl.ds(r + 1, SUB, stride=steps), :]
            else:
                there = pltpu.roll(first[i], SUB - 1, 0)
            east[i, r] = 0.5 * (here[i] + there)
            if i + 1 < rows:
                north[i, r] = 0.5 * (here[i] + here[i + 1])
            else:
                up = 0.5 * (here[i] + pltpu.roll(start_of_row, LANES - 1, 1))
                north[i, r] = jnp.where(edge, jnp.zeros_like(up), up)
            if i == 0:
                start_of_row = here[0]
            here[i] = there if i else here[i]
            if i == 0:
                next_of_row = there
        here[0] = next_of_row


def diffuse_in_place(field, east, north):
    rows, steps = field.shape[:2]

    def one_step(step_index, carry):
        here = [field[i, 0] for i in range(rows)]
        ahead = [pltpu.roll(f, SUB - 1, 0) for f in here]
        before = [
            pltpu.roll(east[i, steps - 1] * (ahead[i] - field[i, steps - 1]), 1, 0)
            for i in range(rows)
        ]
        for r in range(steps):
            there = [field[i, r + 1] if r + 1 < steps else ahead[i] for i in range(rows)]
            up = here[1:] + [pltpu.roll(here[0], LANES - 1, 1)]
            flux_north = [north[i, r] * (up[i] - here[i]) for i in range(rows)]
            down = [pltpu.roll(flux_north[-1], 1, 1)] + flux_north[:-1]
            for i in range(rows):
                flux_east = east[i, r] * (there[i] - here[i])
                field[i, r] = here[i] + ((flux_east - before[i]) + (flux_north[i] - down[i]))
                before[i] = flux_east
            here = there
        return carry

    lax.fori_loop(0, ITERS, one_step, 0)


def spread_out(control_ref, diff_ref, a_ref, b_ref, east, north, field, turned, flat):
    planes, lon, lat = control_ref.shape
    rows, steps = field.shape[:2]
    blocks = lat // rows
    tiles = turned.shape[0]
    turned[tiles - 1] = jnp.zeros(turned.shape[1:], jnp.float32)
    flat[:, (tiles - 1) * LANES :, :] = jnp.zeros((rows, LANES, LANES), jnp.float32)
    half = tiles // 2
    coefficients(diff_ref, east, north, turned, flat)
    for q in range(planes):
        for start, width in blocks_of(lon):
            turned[start // LANES, lat * q : lat * q + lat, :width] = control_ref[
                q, start : start + width, :
            ].T
    for i in range(rows):
        for start, width in blocks_of(lon):
            picked = [
                turned[start // LANES, pl.ds(lat * q + i, blocks, stride=rows), :]
                for q in range(planes)
            ]
            flat[i, start : start + LANES, :] = jnp.concatenate(picked, 0).T
        for r in range(steps):
            field[i, r] = flat[i, pl.ds(r, SUB, stride=steps), :]
    diffuse_in_place(field, east, north)
    for i in range(rows):
        for r in range(steps):
            flat[i, pl.ds(r, SUB, stride=steps), :] = field[i, r]
        for start, width in blocks_of(lon):
            block = flat[i, start : start + LANES, :].T
            out_ref, tile = (a_ref, b_ref)[start // LANES // half], start // LANES % half
            for q in range(planes):
                row = (tile * planes + q) * rows + i
                out_ref[pl.ds(row, blocks, stride=half * planes * rows), :] = block[
                    q * blocks : (q + 1) * blocks, :
                ]


def gather_in(a_ref, b_ref, control_ref, east, north, out_ref, field, turned, flat):
    planes, lon, lat = control_ref.shape
    rows, steps = field.shape[:2]
    blocks = lat // rows
    half = turned.shape[0] // 2
    for i in range(rows):
        for start, width in blocks_of(lon):
            in_ref, tile = (a_ref, b_ref)[start // LANES // half], start // LANES % half
            picked = [
                in_ref[
                    pl.ds((tile * planes + q) * rows + i, blocks, stride=half * planes * rows), :
                ]
                for q in range(planes)
            ]
            flat[i, start : start + LANES, :] = jnp.concatenate(picked, 0).T
        for r in range(steps):
            field[i, r] = flat[i, pl.ds(r, SUB, stride=steps), :]
    diffuse_in_place(field, east, north)
    for i in range(rows):
        for r in range(steps):
            flat[i, pl.ds(r, SUB, stride=steps), :] = field[i, r]
        for start, width in blocks_of(lon):
            block = flat[i, start : start + LANES, :].T
            for q in range(planes):
                turned[start // LANES, pl.ds(lat * q + i, blocks, stride=rows), :] = block[
                    q * blocks : (q + 1) * blocks, :
                ]
    for q in range(planes):
        for start, width in blocks_of(lon):
            back = turned[start // LANES, lat * q : lat * q + lat, :].T
            out_ref[q, start : start + width, :] = (
                control_ref[q, start : start + width, :] + back[:width, :]
            )


def prepare(core_ref, filter_ref, table_ref, count_ref, kind_ref, band_ref, band_t_ref, weight_ref):
    levels = filter_ref.shape[0]
    flat = band_ref.shape[0]
    rows = flat // levels
    kinds, columns = table_ref.shape
    lon = count_ref.shape[1]
    own = weight_ref.shape[0]
    variables = columns // levels
    share = own // variables // rows
    spread = ones_where(iota((flat, levels), 0) // rows == iota((flat, levels), 1))
    spread_t = ones_where(iota((levels, flat), 1) // rows == iota((levels, flat), 0))
    same = lax.rem(iota((flat, flat), 0), rows) == lax.rem(iota((flat, flat), 1), rows)
    weight = filter_ref[...]
    band_ref[...] = jnp.where(same, dot(dot(spread, weight), spread_t), 0.0)
    band_t_ref[...] = jnp.where(same, dot(dot(spread, weight, ((1,), (1,))), spread_t), 0.0)
    row = iota((own, columns), 0)
    column = (
        row // (share * rows) * levels
        + core_ref[0] * share
        + lax.rem(row // rows, share)
    )
    picked = dot(ones_where(column == iota((own, columns), 1)), table_ref[...], ((1,), (1,)))
    wide = kinds * rows
    each = ones_where(iota((kinds, wide), 1) // rows == iota((kinds, wide), 0))
    match = lax.rem(iota((own, wide), 0), rows) == lax.rem(iota((own, wide), 1), rows)
    table = jnp.where(match, dot(picked, each), 0.0)
    repeat = ones_where(lax.rem(iota((wide, rows), 0), rows) == iota((wide, rows), 1))
    kind = dot(repeat, kind_ref[...].astype(jnp.float32))
    count = dot(repeat, count_ref[...].astype(jnp.float32))
    which = (iota((wide, lon), 0) // rows).astype(jnp.float32)
    weight_ref[:, :lon] = dot(table, jnp.where(kind == which, count, 0.0))
    weight_ref[:, lon:] = jnp.zeros((own, weight_ref.shape[1] - lon), jnp.float32)


def relayout(perturb_ref, out_ref):
    levels, rows, lon = perturb_ref.shape
    out_ref[:, lon:] = jnp.zeros((levels * rows, out_ref.shape[1] - lon), jnp.float32)
    pair = SUB // rows
    for t in range(levels // pair):
        out_ref[SUB * t : SUB * t + SUB, :lon] = jnp.concatenate(
            [perturb_ref[pair * t + u] for u in range(pair)], 0
        )


def partial_sums(offset, core_ref, band_ref, pieces_ref, perturb_ref, send_ref, keep_ref, filtered):
    devices, tiles, height = pieces_ref.shape[:3]
    width = tiles * LANES
    members, variables, flat = perturb_ref.shape[:3]
    piece = height // members
    half = flat // 2
    for k in range(members):
        mine = [
            pieces_ref[:, t, piece * k : piece * k + piece, :].reshape(flat, LANES)
            for t in range(tiles)
        ]
        filtered[k] = dot(band_ref[...], jnp.concatenate(mine, 1))
    core = core_ref[0]
    for side, out_ref in enumerate((send_ref, keep_ref)):
        base = (core if side else 1 - core) * half

        def body(t, carry, out_ref=out_ref, base=base):
            at = pl.ds(pl.multiple_of(base + t * SUB, SUB), SUB)
            fields = [filtered[k, at, :] for k in range(members)]
            for v in range(variables):
                total = perturb_ref[0, v, at, offset : offset + width] * fields[0]
                for k in range(1, members):
                    total = total + perturb_ref[k, v, at, offset : offset + width] * fields[k]
                out_ref[pl.ds(pl.multiple_of(v * half + t * SUB, SUB), SUB), :] = total
            return carry

        lax.fori_loop(0, half // SUB, body, 0)


def lift(offset, core_ref, band_ref, own_ref, other_ref, perturb_ref, out_ref, adjoint):
    devices, tiles, height = out_ref.shape[:3]
    width = tiles * LANES
    members, variables, flat = perturb_ref.shape[:3]
    piece = height // members
    half = flat // 2
    core = core_ref[0]
    for side, weighted in enumerate((own_ref, other_ref)):
        base = (core if side == 0 else 1 - core) * half

        def body(t, carry, weighted=weighted, base=base):
            at = pl.ds(pl.multiple_of(base + t * SUB, SUB), SUB)
            parts = [
                weighted[pl.ds(pl.multiple_of(v * half + t * SUB, SUB), SUB), :]
                for v in range(variables)
            ]
            for k in range(members):
                total = perturb_ref[k, 0, at, offset : offset + width] * parts[0]
                for v in range(1, variables):
                    total = total + perturb_ref[k, v, at, offset : offset + width] * parts[v]
                adjoint[k, at, :] = total
            return carry

        lax.fori_loop(0, half // SUB, body, 0)
    for k in range(members):
        whole = dot(band_ref[...], adjoint[k])
        for t in range(tiles):
            out_ref[:, t, piece * k : piece * k + piece, :] = whole[
                :, t * LANES : (t + 1) * LANES
            ].reshape(devices, piece, LANES)


def call(kernel, out_shape, scratch, flops, moved, smem_first=False, limit=16):
    def run(*args):
        specs = [VMEM] * len(args)
        if smem_first:
            specs[0] = SMEM
        return pl.pallas_call(
            kernel,
            out_shape=out_shape,
            in_specs=specs,
            out_specs=jax.tree.map(lambda _: VMEM, out_shape),
            scratch_shapes=scratch,
            cost_estimate=pl.CostEstimate(flops=flops, bytes_accessed=moved, transcendentals=0),
            compiler_params=pltpu.CompilerParams(vmem_limit_bytes=limit << 20),
        )(*args)

    return run


def f32(*shape):
    return jax.ShapeDtypeStruct(shape, jnp.float32)


def local(control, perturb, obs_count, obs_kind, obs_table, band_filter, diffusivity):
    members, level_planes, lat, lon = control.shape
    variables, levels, rows = perturb.shape[1:4]
    devices = lax.axis_size("wide")
    planes = members * level_planes
    steps = lon // SUB
    flat = levels * rows
    half = flat // 2
    padded = -(-lon // (2 * LANES)) * 2 * LANES
    width = padded // 2
    height = planes * rows
    control_t = jnp.swapaxes(control, 2, 3).reshape(planes, lon, lat)
    diff_t = jnp.swapaxes(diffusivity, 0, 1)
    core = (lax.axis_index("mem") % 2).astype(jnp.int32).reshape(1)

    coefs = f32(rows, steps, SUB, LANES)
    field = pltpu.VMEM(coefs.shape, jnp.float32)
    tiles = width // LANES
    turned = pltpu.VMEM((2 * tiles, planes * lat, LANES), jnp.float32)
    flat_field = pltpu.VMEM((rows, padded, LANES), jnp.float32)
    work = planes * lat * lon * ITERS * 8
    size = planes * lat * lon * 4

    sent = f32(devices * tiles * height, LANES)
    sent_a, sent_b, east, north = call(
        spread_out, [sent, sent, coefs, coefs], [field, turned, flat_field], work, 2 * size, limit=20
    )(control_t, diff_t)

    def exchange(sent):
        return lax.all_to_all(sent.reshape(devices, tiles, height, LANES), "wide", 0, 0, tiled=True)

    pieces = [exchange(sent_a), exchange(sent_b)]

    band, band_t, weights = call(
        prepare,
        [f32(flat, flat), f32(flat, flat), f32(variables * half, padded)],
        [],
        1 << 28,
        4 << 20,
        True,
    )(core, band_filter, obs_table, obs_count, obs_kind)
    perturb_rows = pl.pallas_call(
        relayout,
        out_shape=f32(members * variables, flat, padded),
        grid=(members * variables,),
        in_specs=[pl.BlockSpec((None, levels, rows, lon), lambda g: (g, 0, 0, 0))],
        out_specs=pl.BlockSpec((None, flat, padded), lambda g: (g, 0, 0)),
        cost_estimate=pl.CostEstimate(flops=1 << 20, bytes_accessed=6 * size, transcendentals=0),
        compiler_params=pltpu.CompilerParams(vmem_limit_bytes=8 << 20),
    )(perturb.reshape(members * variables, levels, rows, lon))
    perturb_rows = perturb_rows.reshape(members, variables, flat, padded)

    other_core = [(i, i ^ 1) for i in range(4)]
    next_chip = [(i, i ^ 2) for i in range(4)]
    part = f32(variables * half, width)
    lifted = []
    for h in range(2):
        offset = h * width

        def sums(*refs, offset=offset):
            partial_sums(offset, *refs)

        def lifting(*refs, offset=offset):
            lift(offset, *refs)

        scratch = [pltpu.VMEM((members, flat, width), jnp.float32)]
        send, keep = call(sums, [part, part], scratch, 1 << 29, 4 * size, True)(
            core, band, pieces[h], perturb_rows
        )
        on_chip = keep + lax.ppermute(send, "mem", other_core)
        total = on_chip + lax.ppermute(on_chip, "mem", next_chip)
        own = weights[:, offset : offset + width] * total
        other = lax.ppermute(own, "mem", other_core)
        out = call(lifting, f32(devices, tiles, height, LANES), scratch, 1 << 29, 4 * size, True)(
            core, band_t, own, other, perturb_rows
        )
        lifted.append(exchange(out).reshape(sent.shape))

    out = call(
        gather_in, f32(planes, lon, lat), [field, turned, flat_field], work, 3 * size, limit=20
    )(*lifted, control_t, east, north)
    return jnp.swapaxes(out.reshape(members, level_planes, lon, lat), 2, 3)


def solution(mesh):
    placed = (
        P("mem", "wide", None, None),
        P("mem", None, None, "wide", None),
        P("wide", None),
        P("wide", None),
        P(),
        P(),
        P(),
    )
    return jax.shard_map(
        local, mesh=mesh, in_specs=placed, out_specs=P("mem", "wide", None, None), check_vma=False
    )
```

time: 240 us -> 152 us (0.63)
  other arithmetic: 64.4 us -> 1.48 us
  blocking collectives: 94 us -> 45.4 us
  Pallas kernels: 0 us -> 32.3 us
  local copies, waits for them, and re-layouts: 42.9 us -> 15.5 us
  waiting for transfers between devices: 28.2 us -> 45.8 us
  starting transfers between devices: 3.76 us -> 10.9 us
  matrix products: 3.85 us -> 0 us
    all_to_all x3 -> x2, blocking collectives: 94 us -> 45.4 us  [exchange(): lax.all_to_all(sent.reshape(devices, tiles, height, LANES), 'wide', 0, 0,...]
    add x33 -> x2, other arithmetic: 41.5 us -> 1.29 us  [local(): on_chip = keep + lax.ppermute(send, 'mem', other_core)]
    pallas_call x0 -> x8, Pallas kernels: none -> 32.3 us  [the longest x7 31.8 us: run(): pl.pallas_call(kernel, out_shape=out_shape, in_specs=specs, out_specs=jax...]
    ppermute x0 -> x6, waiting for transfers between devices: none -> 30.1 us  [the longest x2 26.2 us: local(): total = on_chip + lax.ppermute(on_chip, 'mem', next_chip)]
    slice x182 -> x0, local copies, waits for them, and re-layouts: 28.4 us -> none  [the longest x64 9.45 us: one_step(): flux_east = east_edge * (jnp.roll(field_now, -1, axis=-1) - field_now)]
    mul x32 -> x1, other arithmetic: 16.1 us -> 0.2 us  [local(): own = weights[:, offset:offset + width] * total]
    all_to_all x1 -> x2, waiting for transfers between devices: 28.2 us -> 15.7 us  [exchange(): lax.all_to_all(sent.reshape(devices, tiles, height, LANES), 'wide', 0, 0,...]
    unnamed x23 -> x38, local copies, waits for them, and re-layouts: 6.59 us -> 15.5 us
  transfers between devices with their start and end apart: 1 -> 8, of which waited for: 1 -> 6; matrix products, arithmetic and copies ran while one was open for 0% -> 1% of each run, Pallas kernels for 0% -> 5%
where the time goes in v2:
time: 152 us
  waiting for transfers between devices  45.8 us (30%)
  blocking collectives  45.4 us (30%)
  Pallas kernels  32.3 us (21%)
  local copies, waits for them, and re-layouts  15.5 us (10%)
  starting transfers between devices  10.9 us (7%)
    all_to_all x2, blocking collectives, exchange(): lax.all_to_all(sent.reshape(devices, tiles, height, LANES), 'wide', 0, 0,...  45.4 us
    pallas_call x7, Pallas kernels, run(): pl.pallas_call(kernel, out_shape=out_shape, in_specs=specs, out_specs=jax...  31.8 us
    ppermute x2, waiting for transfers between devices, local(): total = on_chip + lax.ppermute(on_chip, 'mem', next_chip)  26.2 us
    all_to_all x2, waiting for transfers between devices, exchange(): lax.all_to_all(sent.reshape(devices, tiles, height, LANES), 'wide', 0, 0,...  15.7 us
    unnamed x38, local copies, waits for them, and re-layouts  15.5 us
    all_to_all x2, starting transfers between devices, exchange(): lax.all_to_all(sent.reshape(devices, tiles, height, LANES), 'wide', 0, 0,...  8.48 us
    ppermute x2, waiting for transfers between devices, local(): other = lax.ppermute(own, 'mem', other_core)  3.98 us
  transfers between devices with their start and end apart: 8, of which 6 were waited for; matrix products, arithmetic and copies ran while one was open for 1% of the time, Pallas kernels for 5%

profile of v2, /device:TPU:0, one launch (start us, length us, event | category | flops | bytes accessed | tf_op | source)
XLA Modules:
  0.0 151.6 jit_solution(9837823400699084314)
XLA Ops:
  0.0 0.0 copy-start.3
  0.0 1.4 copy-done.3
  1.4 0.0 copy-start.12
  1.4 1.0 copy-done.12
  2.4 11.8 %shard_map.74 = (f32[1536,128]{1,0:T(8,128)S(1)}, f32[1536,128]{1,0:T(8,128)}, f32[4,90,8,128]{3,2,1,0:T(8,128)S(1)}, f32[4,90,8,128]{3,2,1,0:T(8,128)S(1)}) custom-call(f32[4,720,128]{2,1,0:T(8,128)S(1)} %bitcast.20, f32[720,128]{1,0:T(8,128)S(1)} %bitcast.26), custom_call_target="tpu_custom_call" | custom-call | flops 47185920 | bytes 2949120 | tf_op jit(solution)/shard_map/pallas_call | solution.py:275
  14.1 0.0 copy-start.6
  14.1 1.1 copy-done.6
  15.2 0.0 copy-start.8
  15.2 1.2 copy-done.8
  16.4 26.0 %all_to_all.20.refs_2_ = f32[32,3,16,128]{3,2,1,0:T(8,128)S(1)} all-to-all(f32[32,3,16,128]{3,2,1,0:T(8,128)S(1)} %bitcast.25), channel_id=1, replica_groups=mesh['mem'=4,'wide'=32] {'wide'}, dimensions={0} | all-to-all | bytes 1572864 | tf_op jit(solution)/shard_map/all_to_all | solution.py:321
  42.4 4.3 %all-to-all-start.2 = ((f32[32,3,16,128]{3,2,1,0:T(8,128)}), f32[32,3,16,128]{3,2,1,0:T(8,128)S(1)}, u32[]{:S(2)}, u32[]{:S(2)}) async-start(f32[32,3,16,128]{3,2,1,0:T(8,128)} %bitcast.8), calls=%async_computation.2 | async-start | bytes 1572864 | tf_op jit(solution)/shard_map/all_to_all | solution.py:321
  46.7 0.0 copy-start.5
  46.7 2.3 %copy-done.5 = f32[2,3,64,4,720]{4,3,2,1,0:T(4,128)S(1)} copy-done((f32[2,3,64,4,720]{4,3,2,1,0:T(4,128)S(1)}, f32[2,3,64,4,720]{4,3,2,1,0:T(4,128)}, u32[]{:S(2)}) %copy-start.5) | copy-done | bytes 4423704
  49.0 0.0 copy-start.13
  49.0 0.0 copy-start.14
  49.0 0.0 copy-start.15
  49.0 0.0 copy-start.16
  49.0 0.5 shard_map.75
  49.5 0.0 copy-start
  49.6 0.2 copy-done.13
  49.8 0.0 copy-done.14
  49.8 0.0 copy-done.15
  49.8 0.0 copy-done.16
  49.8 2.8 %shard_map.73 = (f32[256,256]{1,0:T(8,128)S(1)}, f32[256,256]{1,0:T(8,128)S(1)}, f32[384,768]{1,0:T(8,128)S(1)}) custom-call(s32[1]{0:T(128)} %bitcast.core_ref.refs_0_, f32[64,64]{1,0:T(8,128)S(1)} %copy-done.13, f32[8,192]{1,0:T(8,128)S(1)} %copy-done.16, s32[4,720]{1,0:T(4,128)S(1)} %copy-done.14, s32[4,720]{1,0:T(4,128)S(1)} %copy-done.15), custom_call_target="tpu_custom_call" | custom-call | flops 268435456 | bytes 4194304 | tf_op jit(solution)/shard_map/pallas_call | solution.py:275
  52.7 2.2 %shard_map.76 = (f32[384,384]{1,0:T(8,128)}, f32[384,384]{1,0:T(8,128)S(1)}) custom-call(s32[1]{0:T(128)} %bitcast.core_ref.refs_0_, f32[256,256]{1,0:T(8,128)S(1)} %get-tuple-element.18.refs_1_, f32[32,3,16,128]{3,2,1,0:T(8,128)S(1)} %all_to_all.20.refs_2_, f32[2,3,256,768]{3,2,1,0:T(8,128)S(1)} %bitcast.14), custom_call_target="tpu_custom_call" | custom-call | flops 536870912 | bytes 5898240 | tf_op jit(solution)/shard_map/pallas_call | solution.py:275
  54.9 0.0 copy-done
  54.9 0.0 copy-start.10
  54.9 0.9 copy-done.10
  55.7 0.0 collective-permute-start
  55.7 5.8 %all-to-all-done.2.refs_2_ = f32[32,3,16,128]{3,2,1,0:T(8,128)S(1)} async-done(((f32[32,3,16,128]{3,2,1,0:T(8,128)}), f32[32,3,16,128]{3,2,1,0:T(8,128)S(1)}, u32[]{:S(2)}, u32[]{:S(2)}) %all-to-all-start.2) | async-done | bytes 786464 | tf_op jit(solution)/shard_map/all_to_all | solution.py:321
  61.5 0.0 copy-start.1
  61.6 2.3 %copy-done.1 = f32[6,256,768]{2,1,0:T(8,128)S(1)} copy-done((f32[6,256,768]{2,1,0:T(8,128)S(1)}, f32[6,256,768]{2,1,0:T(8,128)}, u32[]{:S(2)}) %copy-start.1) | copy-done | bytes 4718616
  63.9 0.0 copy-start.11
  63.9 0.0 slice-start
  63.9 1.4 shard_map.78
  65.3 0.1 collective-permute-start.3
  65.4 0.0 collective-permute-done
  65.4 0.0 copy-done.11
  65.4 0.0 slice-start.1
  65.4 1.2 add.17
  66.6 1.1 collective-permute-start.1
  67.7 0.0 collective-permute-done.3
  67.7 0.1 add.19
  67.8 1.1 collective-permute-start.4
  68.9 14.0 %collective-permute-done.1 = f32[384,384]{1,0:T(8,128)S(1)} collective-permute-done((f32[384,384]{1,0:T(8,128)S(1)}, f32[384,384]{1,0:T(8,128)S(1)}, u32[]{:S(2)}, u32[]{:S(2)}) %collective-permute-start.1) | collective-permute-done | bytes 589856 | tf_op jit(solution)/shard_map/ppermute | solution.py:362
  82.9 12.1 %collective-permute-done.4 = f32[384,384]{1,0:T(8,128)S(1)} collective-permute-done((f32[384,384]{1,0:T(8,128)S(1)}, f32[384,384]{1,0:T(8,128)S(1)}, u32[]{:S(2)}, u32[]{:S(2)}) %collective-permute-start.4) | collective-permute-done | bytes 589856 | tf_op jit(solution)/shard_map/ppermute | solution.py:362
  95.0 0.2 add_multiply_fusion
  95.2 0.1 collective-permute-start.5
  95.3 2.0 %collective-permute-done.5.refs_3_ = f32[384,384]{1,0:T(8,128)S(1)} collective-permute-done((f32[384,384]{1,0:T(8,128)S(1)}, f32[384,384]{1,0:T(8,128)S(1)}, u32[]{:S(2)}, u32[]{:S(2)}) %collective-permute-start.5) | collective-permute-done | bytes 589856 | tf_op jit(solution)/shard_map/ppermute | solution.py:364
  97.3 0.0 slice-done
  97.3 0.0 slice-done.1
  97.3 2.3 %shard_map.79 = f32[32,3,16,128]{3,2,1,0:T(8,128)} custom-call(s32[1]{0:T(128)} %bitcast.core_ref.refs_0_, f32[256,256]{1,0:T(8,128)S(1)} %get-tuple-element.16.refs_1_, f32[384,384]{1,0:T(8,128)S(1)} %get-tuple-element.27.refs_2_, f32[384,384]{1,0:T(8,128)S(1)} %collective-permute-done.5.refs_3_, f32[2,3,256,768]{3,2,1,0:T(8,128)S(1)} %bitcast.18), custom_call_target="tpu_custom_call" | custom-call | flops 536870912 | bytes 5898240 | tf_op jit(solution)/shard_map/pallas_call | solution.py:275
  99.6 4.2 %all-to-all-start.3 = ((f32[32,3,16,128]{3,2,1,0:T(8,128)}), f32[32,3,16,128]{3,2,1,0:T(8,128)S(1)}, u32[]{:S(2)}, u32[]{:S(2)}) async-start(f32[32,3,16,128]{3,2,1,0:T(8,128)} %shard_map.79), calls=%async_computation.3 | async-start | bytes 1572864 | tf_op jit(solution)/shard_map/all_to_all | solution.py:321
  103.8 0.1 collective-permute-start.2
  103.9 2.0 %collective-permute-done.2.refs_3_ = f32[384,384]{1,0:T(8,128)S(1)} collective-permute-done((f32[384,384]{1,0:T(8,128)S(1)}, f32[384,384]{1,0:T(8,128)S(1)}, u32[]{:S(2)}, u32[]{:S(2)}) %collective-permute-start.2) | collective-permute-done | bytes 589856 | tf_op jit(solution)/shard_map/ppermute | solution.py:364
  105.9 2.3 %copy-done.2 = f32[6,256,768]{2,1,0:T(8,128)S(1)} copy-done((f32[6,256,768]{2,1,0:T(8,128)S(1)}, f32[6,256,768]{2,1,0:T(8,128)}, u32[]{:S(2)}) %copy-start.2) | copy-done | bytes 4718616
  108.3 1.4 shard_map.77
  109.7 0.0 copy-start.4
  109.7 9.8 %all-to-all-done.3 = f32[32,3,16,128]{3,2,1,0:T(8,128)S(1)} async-done(((f32[32,3,16,128]{3,2,1,0:T(8,128)}), f32[32,3,16,128]{3,2,1,0:T(8,128)S(1)}, u32[]{:S(2)}, u32[]{:S(2)}) %all-to-all-start.3) | async-done | bytes 786464 | tf_op jit(solution)/shard_map/all_to_all | solution.py:321
  119.5 19.4 %all_to_all.21 = f32[32,3,16,128]{3,2,1,0:T(8,128)S(1)} all-to-all(f32[32,3,16,128]{3,2,1,0:T(8,128)S(1)} %shard_map.77), channel_id=1, replica_groups=mesh['mem'=4,'wide'=32] {'wide'}, dimensions={0} | all-to-all | bytes 1572864 | tf_op jit(solution)/shard_map/all_to_all | solution.py:321
  138.9 0.0 copy-done.4
  138.9 1.4 copy-done.7
  140.3 1.4 copy-done.9
  141.7 10.0 %shard_map.80 = f32[4,720,128]{2,1,0:T(8,128)} custom-call(f32[1536,128]{1,0:T(8,128)S(1)} %bitcast.24, f32[1536,128]{1,0:T(8,128)S(1)} %bitcast.23, f32[4,720,128]{2,1,0:T(8,128)S(1)} %bitcast.21, f32[4,90,8,128]{3,2,1,0:T(8,128)S(1)} %copy-done.7, f32[4,90,8,128]{3,2,1,0:T(8,128)S(1)} %copy-done.9), custom_call_target="tpu_custom_call" | custom-call | flops 47185920 | bytes 4423680 | tf_op jit(solution)/shard_map/pallas_call | solution.py:275
  (4 shorter events, 0.0 us)
Async XLA Ops:
  0.0 1.4 copy-start.3
  1.4 1.0 copy-start.12
  14.1 1.1 copy-start.6
  15.2 1.2 copy-start.8
  42.4 19.1 %all-to-all-start.2 = ((f32[32,3,16,128]{3,2,1,0:T(8,128)}), f32[32,3,16,128]{3,2,1,0:T(8,128)S(1)}, u32[]{:S(2)}, u32[]{:S(2)}) async-start(f32[32,3,16,128]{3,2,1,0:T(8,128)} %bitcast.8), calls=%async_computation.2 | async-start | bytes 1572864 | tf_op jit(solution)/shard_map/all_to_all | solution.py:321
  46.7 2.3 %copy-start.5 = (f32[2,3,64,4,720]{4,3,2,1,0:T(4,128)S(1)}, f32[2,3,64,4,720]{4,3,2,1,0:T(4,128)}, u32[]{:S(2)}) copy-start(f32[2,3,64,4,720]{4,3,2,1,0:T(4,128)} %param.8) | copy-start | bytes 13271044
  49.0 0.8 copy-start.13
  49.0 0.8 copy-start.14
  49.0 0.8 copy-start.15
  49.0 0.8 copy-start.16
  49.5 5.3 %copy-start = (f32[6,256,768]{2,1,0:T(8,128)}, f32[6,256,768]{2,1,0:T(8,128)S(1)}, u32[]{:S(2)}) copy-start(f32[6,256,768]{2,1,0:T(8,128)S(1)} %shard_map.75) | copy-start | bytes 14155780
  54.9 0.9 copy-start.10
  55.7 9.6 %collective-permute-start = (f32[384,384]{1,0:T(8,128)}, f32[384,384]{1,0:T(8,128)}, u32[]{:S(2)}, u32[]{:S(2)}) collective-permute-start(f32[384,384]{1,0:T(8,128)} %get-tuple-element.21), channel_id=1, source_target_pairs={{0,32},{32,0},{64,96},{96,64},{1,33},{33,1},{65,97},{97,65},{2,34}... | collective-permute-start | bytes 1769480 | tf_op jit(solution)/shard_map/ppermute | solution.py:361
  61.5 2.3 %copy-start.1 = (f32[6,256,768]{2,1,0:T(8,128)S(1)}, f32[6,256,768]{2,1,0:T(8,128)}, u32[]{:S(2)}) copy-start(f32[6,256,768]{2,1,0:T(8,128)} %copy-done) | copy-start | bytes 14155780
  63.9 1.5 copy-start.11
  63.9 33.4 %slice-start = ((s8[4718592]{0:T(1024)(128)(4,1)}), s8[4194304]{0:T(1024)(128)(4,1)S(1)}, s32[]{:S(2)}) async-start(s8[4718592]{0:T(1024)(128)(4,1)} %bitcast.16), calls=%async_computation.4 | async-start | bytes 8388608
  65.3 2.4 %collective-permute-start.3 = (f32[384,384]{1,0:T(8,128)S(1)}, f32[384,384]{1,0:T(8,128)S(1)}, u32[]{:S(2)}, u32[]{:S(2)}) collective-permute-start(f32[384,384]{1,0:T(8,128)S(1)} %get-tuple-element.24), channel_id=1, source_target_pairs={{0,32},{32,0},{64,96},{96,64},{1,33},{33,1},{65,97},{97,65},{2,34}... | collective-permute-start | bytes 1769480 | tf_op jit(solution)/shard_map/ppermute | solution.py:361
  65.4 31.9 %slice-start.1 = ((s8[4718592]{0:T(1024)(128)(4,1)}), s8[524288]{0:T(1024)(128)(4,1)S(1)}, s32[]{:S(2)}) async-start(s8[4718592]{0:T(1024)(128)(4,1)} %bitcast.16), calls=%async_computation.5 | async-start | bytes 1048576
  66.6 16.3 %collective-permute-start.1 = (f32[384,384]{1,0:T(8,128)S(1)}, f32[384,384]{1,0:T(8,128)S(1)}, u32[]{:S(2)}, u32[]{:S(2)}) collective-permute-start(f32[384,384]{1,0:T(8,128)S(1)} %add.17), channel_id=1, source_target_pairs={{0,64},{32,96},{64,0},{96,32},{1,65},{33,97},{65,1},{97,33},{2,66}... | collective-permute-start | bytes 1769480 | tf_op jit(solution)/shard_map/ppermute | solution.py:362
  67.8 27.2 %collective-permute-start.4 = (f32[384,384]{1,0:T(8,128)S(1)}, f32[384,384]{1,0:T(8,128)S(1)}, u32[]{:S(2)}, u32[]{:S(2)}) collective-permute-start(f32[384,384]{1,0:T(8,128)S(1)} %add.19), channel_id=1, source_target_pairs={{0,64},{32,96},{64,0},{96,32},{1,65},{33,97},{65,1},{97,33},{2,66}... | collective-permute-start | bytes 1769480 | tf_op jit(solution)/shard_map/ppermute | solution.py:362
  95.2 2.1 %collective-permute-start.5 = (f32[384,384]{1,0:T(8,128)S(1)}, f32[384,384]{1,0:T(8,128)S(1)}, u32[]{:S(2)}, u32[]{:S(2)}) collective-permute-start(f32[384,384]{1,0:T(8,128)S(1)} %get-tuple-element.27.refs_2_), channel_id=1, source_target_pairs={{0,32},{32,0},{64,96},{96,64},{1,33},{33,1},{65,97},{97,65},{2,34}... | collective-permute-start | bytes 1769480 | tf_op jit(solution)/shard_map/ppermute | solution.py:364
  99.6 19.9 %all-to-all-start.3 = ((f32[32,3,16,128]{3,2,1,0:T(8,128)}), f32[32,3,16,128]{3,2,1,0:T(8,128)S(1)}, u32[]{:S(2)}, u32[]{:S(2)}) async-start(f32[32,3,16,128]{3,2,1,0:T(8,128)} %shard_map.79), calls=%async_computation.3 | async-start | bytes 1572864 | tf_op jit(solution)/shard_map/all_to_all | solution.py:321
  103.8 2.1 %collective-permute-start.2 = (f32[384,384]{1,0:T(8,128)S(1)}, f32[384,384]{1,0:T(8,128)S(1)}, u32[]{:S(2)}, u32[]{:S(2)}) collective-permute-start(f32[384,384]{1,0:T(8,128)S(1)} %get-tuple-element.28.refs_2_), channel_id=1, source_target_pairs={{0,32},{32,0},{64,96},{96,64},{1,33},{33,1},{65,97},{97,65},{2,34}... | collective-permute-start | bytes 1769480 | tf_op jit(solution)/shard_map/ppermute | solution.py:364
  105.9 2.3 %copy-start.2 = (f32[6,256,768]{2,1,0:T(8,128)S(1)}, f32[6,256,768]{2,1,0:T(8,128)}, u32[]{:S(2)}) copy-start(f32[6,256,768]{2,1,0:T(8,128)} %copy-done) | copy-start | bytes 14155780
  109.7 29.3 %copy-start.4 = (f32[2,2,128,720]{2,3,1,0:T(8,128)S(1)}, f32[2,2,128,720]{2,3,1,0:T(8,128)}, u32[]{:S(2)}) copy-start(f32[2,2,128,720]{2,3,1,0:T(8,128)} %param.7) | copy-start | bytes 4423684
  138.9 1.4 copy-start.7
  140.3 1.4 copy-start.9

commit v3 on v2

v3 whole, which is shorter than its diff:
```python
import jax
import jax.numpy as jnp
from jax import lax
from jax.experimental import pallas as pl
from jax.experimental.pallas import tpu as pltpu
from jax.sharding import PartitionSpec as P


ITERS = 16
SUB = 8
LANES = 128
VMEM = pl.BlockSpec(memory_space=pltpu.VMEM)
SMEM = pl.BlockSpec(memory_space=pltpu.SMEM)
HBM = pl.BlockSpec(memory_space=pltpu.HBM)
HIGHEST = lax.Precision.HIGHEST


def dot(a, b, contract=((1,), (0,))):
    return lax.dot_general(
        a, b, (contract, ((), ())), precision=HIGHEST, preferred_element_type=jnp.float32
    )


def iota(shape, dim):
    return lax.broadcasted_iota(jnp.int32, shape, dim)


def ones_where(mask):
    return jnp.where(mask, 1.0, 0.0).astype(jnp.float32)


def blocks_of(lon):
    return [(start, min(LANES, lon - start)) for start in range(0, lon, LANES)]


def coefficients(diff_ref, east, north, turned, flat):
    rows, steps = east.shape[:2]
    lon, lat = diff_ref.shape
    blocks = lat // rows
    copies = LANES // blocks
    for start, width in blocks_of(lon):
        turned[start // LANES, :lat, :width] = diff_ref[start : start + width, :].T
    for i in range(rows):
        for start, width in blocks_of(lon):
            picked = turned[start // LANES, pl.ds(i, blocks, stride=rows), :]
            flat[i, start : start + LANES, :] = jnp.concatenate([picked] * copies, 0).T
    edge = lax.rem(iota((SUB, LANES), 1), blocks) == blocks - 1
    first = [flat[i, pl.ds(0, SUB, stride=steps), :] for i in range(rows)]
    here = list(first)
    for r in range(steps):
        for i in range(rows):
            if r + 1 < steps:
                there = flat[i, pl.ds(r + 1, SUB, stride=steps), :]
            else:
                there = pltpu.roll(first[i], SUB - 1, 0)
            east[i, r] = 0.5 * (here[i] + there)
            if i + 1 < rows:
                north[i, r] = 0.5 * (here[i] + here[i + 1])
            else:
                up = 0.5 * (here[i] + pltpu.roll(start_of_row, LANES - 1, 1))
                north[i, r] = jnp.where(edge, jnp.zeros_like(up), up)
            if i == 0:
                start_of_row = here[0]
            here[i] = there if i else here[i]
            if i == 0:
                next_of_row = there
        here[0] = next_of_row


def diffuse_in_place(field, east, north):
    rows, steps = field.shape[:2]

    def one_step(step_index, carry):
        here = [field[i, 0] for i in range(rows)]
        ahead = [pltpu.roll(f, SUB - 1, 0) for f in here]
        before = [
            pltpu.roll(east[i, steps - 1] * (ahead[i] - field[i, steps - 1]), 1, 0)
            for i in range(rows)
        ]
        for r in range(steps):
            there = [field[i, r + 1] if r + 1 < steps else ahead[i] for i in range(rows)]
            up = here[1:] + [pltpu.roll(here[0], LANES - 1, 1)]
            flux_north = [north[i, r] * (up[i] - here[i]) for i in range(rows)]
            down = [pltpu.roll(flux_north[-1], 1, 1)] + flux_north[:-1]
            for i in range(rows):
                flux_east = east[i, r] * (there[i] - here[i])
                field[i, r] = here[i] + ((flux_east - before[i]) + (flux_north[i] - down[i]))
                before[i] = flux_east
            here = there
        return carry

    lax.fori_loop(0, ITERS, one_step, 0)


def spread_out(
    control_hbm, diff_ref, sent_ref, east_hbm, north_hbm,
    control, east, north, field, turned, flat, sems,
):
    planes, lon, lat = control.shape
    rows, steps = field.shape[:2]
    blocks = lat // rows
    tiles = turned.shape[0]
    fetch = pltpu.make_async_copy(control_hbm, control, sems.at[0])
    fetch.start()
    turned[tiles - 1] = jnp.zeros(turned.shape[1:], jnp.float32)
    flat[:, (tiles - 1) * LANES :, :] = jnp.zeros((rows, LANES, LANES), jnp.float32)
    coefficients(diff_ref, east, north, turned, flat)
    keep_east = pltpu.make_async_copy(east, east_hbm, sems.at[1])
    keep_north = pltpu.make_async_copy(north, north_hbm, sems.at[2])
    keep_east.start()
    keep_north.start()
    fetch.wait()
    for q in range(planes):
        for start, width in blocks_of(lon):
            turned[start // LANES, lat * q : lat * q + lat, :width] = control[
                q, start : start + width, :
            ].T
    for i in range(rows):
        for start, width in blocks_of(lon):
            picked = [
                turned[start // LANES, pl.ds(lat * q + i, blocks, stride=rows), :]
                for q in range(planes)
            ]
            flat[i, start : start + LANES, :] = jnp.concatenate(picked, 0).T
        for r in range(steps):
            field[i, r] = flat[i, pl.ds(r, SUB, stride=steps), :]
    diffuse_in_place(field, east, north)
    for i in range(rows):
        for r in range(steps):
            flat[i, pl.ds(r, SUB, stride=steps), :] = field[i, r]
        for start, width in blocks_of(lon):
            block = flat[i, start : start + LANES, :].T
            for q in range(planes):
                row = (start // LANES * planes + q) * rows + i
                sent_ref[pl.ds(row, blocks, stride=tiles * planes * rows), :] = block[
                    q * blocks : (q + 1) * blocks, :
                ]
    keep_east.wait()
    keep_north.wait()


def gather_in(
    a_ref, b_ref, control_hbm, east_hbm, north_hbm, out_hbm,
    control, east, north, field, turned, flat, sems,
):
    planes, lon, lat = control.shape
    rows, steps = field.shape[:2]
    blocks = lat // rows
    tiles_a = a_ref.shape[0] // (blocks * planes * rows)
    tiles_b = b_ref.shape[0] // (blocks * planes * rows)
    fetches = [
        pltpu.make_async_copy(source, target, sems.at[n])
        for n, (source, target) in enumerate(
            ((east_hbm, east), (north_hbm, north), (control_hbm, control))
        )
    ]
    for fetch in fetches:
        fetch.start()
    for i in range(rows):
        for start, width in blocks_of(lon):
            in_ref, tile, tiles = a_ref, start // LANES, tiles_a
            if tile >= tiles_a:
                in_ref, tile, tiles = b_ref, tile - tiles_a, tiles_b
            picked = [
                in_ref[
                    pl.ds((tile * planes + q) * rows + i, blocks, stride=tiles * planes * rows), :
                ]
                for q in range(planes)
            ]
            flat[i, start : start + LANES, :] = jnp.concatenate(picked, 0).T
        for r in range(steps):
            field[i, r] = flat[i, pl.ds(r, SUB, stride=steps), :]
    for fetch in fetches:
        fetch.wait()
    diffuse_in_place(field, east, north)
    for i in range(rows):
        for r in range(steps):
            flat[i, pl.ds(r, SUB, stride=steps), :] = field[i, r]
        for start, width in blocks_of(lon):
            block = flat[i, start : start + LANES, :].T
            for q in range(planes):
                turned[start // LANES, pl.ds(lat * q + i, blocks, stride=rows), :] = block[
                    q * blocks : (q + 1) * blocks, :
                ]
    stores = []
    for q in range(planes):
        for start, width in blocks_of(lon):
            back = turned[start // LANES, lat * q : lat * q + lat, :].T
            place = pl.ds(start, width)
            control[q, place, :] = control[q, place, :] + back[:width, :]
        stores.append(pltpu.make_async_copy(control.at[q], out_hbm.at[q], sems.at[3 + q]))
        stores[-1].start()
    for store in stores:
        store.wait()


def prepare(core_ref, filter_ref, table_ref, count_ref, kind_ref, band_ref, band_t_ref, *weight_refs):
    levels = filter_ref.shape[0]
    flat = band_ref.shape[0]
    rows = flat // levels
    kinds, columns = table_ref.shape
    lon = count_ref.shape[1]
    own, width = weight_refs[0].shape
    variables = columns // levels
    share = own // variables // rows
    spread = ones_where(iota((flat, levels), 0) // rows == iota((flat, levels), 1))
    spread_t = ones_where(iota((levels, flat), 1) // rows == iota((levels, flat), 0))
    same = lax.rem(iota((flat, flat), 0), rows) == lax.rem(iota((flat, flat), 1), rows)
    weight = filter_ref[...]
    band_ref[...] = jnp.where(same, dot(dot(spread, weight), spread_t), 0.0)
    band_t_ref[...] = jnp.where(same, dot(dot(spread, weight, ((1,), (1,))), spread_t), 0.0)
    row = iota((own, columns), 0)
    column = (
        row // (share * rows) * levels
        + core_ref[0] * share
        + lax.rem(row // rows, share)
    )
    picked = dot(ones_where(column == iota((own, columns), 1)), table_ref[...], ((1,), (1,)))
    wide = kinds * rows
    each = ones_where(iota((kinds, wide), 1) // rows == iota((kinds, wide), 0))
    match = lax.rem(iota((own, wide), 0), rows) == lax.rem(iota((own, wide), 1), rows)
    table = jnp.where(match, dot(picked, each), 0.0)
    repeat = ones_where(lax.rem(iota((wide, rows), 0), rows) == iota((wide, rows), 1))
    kind = dot(repeat, kind_ref[...].astype(jnp.float32))
    count = dot(repeat, count_ref[...].astype(jnp.float32))
    which = (iota((wide, lon), 0) // rows).astype(jnp.float32)
    chosen = jnp.where(kind == which, count, 0.0)
    for h, weight_ref in enumerate(weight_refs):
        used = min(width, lon - h * width)
        if used < width:
            weight_ref[:, used:] = jnp.zeros((own, width - used), jnp.float32)
        weight_ref[:, :used] = dot(table, chosen[:, h * width : h * width + used])


def level_pair(perturb_ref, k, v, level, rows):
    return jnp.concatenate([perturb_ref[k, v, level + u] for u in range(SUB // rows)], 0)


def partial_sums(core_ref, band_ref, pieces_ref, perturb_ref, send_ref, keep_ref, filtered):
    members, variables, levels, rows = perturb_ref.shape[:4]
    flat = levels * rows
    piece = pieces_ref.shape[1] // members
    mine = [
        pieces_ref[:, piece * k : piece * k + piece, :].reshape(flat, LANES)
        for k in range(members)
    ]
    filtered[...] = dot(band_ref[...], jnp.concatenate(mine, 1))
    core = core_ref[0]
    half = flat // 2
    for side, out_ref in enumerate((send_ref, keep_ref)):
        part = core if side else 1 - core
        for t in range(half // SUB):
            at = pl.ds(pl.multiple_of(part * half + t * SUB, SUB), SUB)
            level = part * (levels // 2) + t * (SUB // rows)
            fields = [filtered[at, LANES * k : LANES * (k + 1)] for k in range(members)]
            for v in range(variables):
                total = level_pair(perturb_ref, 0, v, level, rows) * fields[0]
                for k in range(1, members):
                    total = total + level_pair(perturb_ref, k, v, level, rows) * fields[k]
                out_ref[v * half + t * SUB : v * half + t * SUB + SUB, :] = total


def lift(core_ref, band_ref, own_ref, other_ref, perturb_ref, *rest):
    out_ref, adjoint = rest[-2:]
    members, variables, levels, rows = perturb_ref.shape[:4]
    flat = levels * rows
    piece = out_ref.shape[1] // members
    core = core_ref[0]
    half = flat // 2
    for side, weighted in enumerate((own_ref, other_ref)):
        part = core if side == 0 else 1 - core
        for t in range(half // SUB):
            at = pl.ds(pl.multiple_of(part * half + t * SUB, SUB), SUB)
            level = part * (levels // 2) + t * (SUB // rows)
            parts = [
                weighted[v * half + t * SUB : v * half + t * SUB + SUB, :]
                for v in range(variables)
            ]
            for k in range(members):
                total = level_pair(perturb_ref, k, 0, level, rows) * parts[0]
                for v in range(1, variables):
                    total = total + level_pair(perturb_ref, k, v, level, rows) * parts[v]
                adjoint[at, LANES * k : LANES * (k + 1)] = total
    whole = dot(band_ref[...], adjoint[...])
    for k in range(members):
        out_ref[:, piece * k : piece * k + piece, :] = whole[
            :, LANES * k : LANES * (k + 1)
        ].reshape(-1, piece, LANES)


def add_up(keep_ref, got_ref, out_ref):
    out_ref[...] = keep_ref[...] + got_ref[...]


def weigh(weight_ref, on_chip_ref, got_ref, out_ref):
    out_ref[...] = weight_ref[...] * (on_chip_ref[...] + got_ref[...])


def call(kernel, out_shape, flops, moved, ins=None, outs=None, scratch=(), limit=8, **grid):
    def run(*args):
        return pl.pallas_call(
            kernel,
            out_shape=out_shape,
            in_specs=ins or [VMEM] * len(args),
            out_specs=outs or jax.tree.map(lambda _: VMEM, out_shape),
            scratch_shapes=scratch,
            cost_estimate=pl.CostEstimate(flops=flops, bytes_accessed=moved, transcendentals=0),
            compiler_params=pltpu.CompilerParams(vmem_limit_bytes=limit << 20),
            **grid,
        )(*args)

    return run


def f32(*shape):
    return jax.ShapeDtypeStruct(shape, jnp.float32)


def local(control, perturb, obs_count, obs_kind, obs_table, band_filter, diffusivity):
    members, level_planes, lat, lon = control.shape
    variables, levels, rows = perturb.shape[1:4]
    devices = lax.axis_size("wide")
    planes = members * level_planes
    steps = lon // SUB
    flat = levels * rows
    half = flat // 2
    chunk = 2
    tiles = -(-lon // (chunk * LANES)) * chunk
    width = chunk * LANES
    height = planes * rows
    control_t = jnp.swapaxes(control, 2, 3).reshape(planes, lon, lat)
    control_t = pltpu.with_memory_space_constraint(control_t, pltpu.HBM)
    diff_t = jnp.swapaxes(diffusivity, 0, 1)
    core = (lax.axis_index("mem") % 2).astype(jnp.int32).reshape(1)

    coefs = f32(rows, steps, SUB, LANES)
    vmem = [
        (planes, lon, lat),
        coefs.shape,
        coefs.shape,
        coefs.shape,
        (tiles, planes * lat, LANES),
        (rows, tiles * LANES, LANES),
    ]
    vmem = [pltpu.VMEM(shape, jnp.float32) for shape in vmem]
    work = planes * lat * lon * ITERS * 8
    size = planes * lat * lon * 4

    sent, east, north = call(
        spread_out,
        [f32(devices * tiles * height, LANES)] + [pltpu.HBM(coefs.shape, coefs.dtype)] * 2,
        work,
        2 * size,
        [HBM, VMEM],
        [VMEM, HBM, HBM],
        [*vmem, pltpu.SemaphoreType.DMA((3,))],
        20,
    )(control_t, diff_t)
    east, north = (pltpu.with_memory_space_constraint(e, pltpu.HBM) for e in (east, north))

    def exchange(sent):
        return lax.all_to_all(sent.reshape(devices, -1, height, LANES), "wide", 0, 0, tiled=True)

    pieces = exchange(sent)

    part = f32(variables * half, width)
    band, band_t, *weights = call(
        prepare,
        [f32(flat, flat), f32(flat, flat)] + [part] * (tiles // chunk),
        1 << 28,
        4 << 20,
        [SMEM] + [VMEM] * 4,
    )(core, band_filter, obs_table, obs_count, obs_kind)

    other_core = [(i, i ^ 1) for i in range(4)]
    next_chip = [(i, i ^ 2) for i in range(4)]
    perturb = pltpu.with_memory_space_constraint(perturb, pltpu.HBM)
    in_band = pl.BlockSpec((flat, flat), lambda g: (0, 0))
    in_part = pl.BlockSpec((variables * half, LANES), lambda g: (0, g))
    scratch = [pltpu.VMEM((flat, members * LANES), jnp.float32)]
    home = None
    lifted = []
    for h in range(tiles // chunk):
        in_piece = pl.BlockSpec(
            (devices, None, height, LANES), lambda g, h=h: (0, h * chunk + g, 0, 0)
        )
        in_perturb = pl.BlockSpec(
            (members, variables, levels, rows, LANES),
            lambda g, h=h: (0, 0, 0, 0, h * chunk + g),
        )
        send, keep = call(
            partial_sums,
            [part, part],
            1 << 29,
            4 * size,
            [SMEM, in_band, in_piece, in_perturb],
            [in_part, in_part],
            scratch,
            grid=(chunk,),
        )(core, band, pieces, perturb)
        got = lax.ppermute(send, "mem", other_core)
        on_chip = call(add_up, part, 1 << 18, size)(keep, got)
        got = lax.ppermute(on_chip, "mem", next_chip)
        own = call(weigh, part, 1 << 18, size)(weights[h], on_chip, got)
        other = lax.ppermute(own, "mem", other_core)
        first, last = h < 2, h != 1
        count = chunk if h == 0 else tiles - chunk
        out_piece = pl.BlockSpec(
            (devices, None, height, LANES), lambda g, h=h: (0, max(h - 1, 0) * chunk + g, 0, 0)
        )
        home = call(
            lift,
            f32(devices, count, height, LANES),
            1 << 29,
            4 * size,
            [SMEM, in_band, in_part, in_part, in_perturb]
            + ([] if first else [pl.BlockSpec(memory_space=pl.ANY)]),
            out_piece,
            scratch,
            grid=(chunk,),
            input_output_aliases={} if first else {5: 0},
        )(core, band_t, own, other, perturb, *([] if first else [home]))
        if last:
            lifted.append(exchange(home).reshape(-1, LANES))

    out = call(
        gather_in,
        pltpu.HBM((planes, lon, lat), jnp.float32),
        work,
        3 * size,
        [VMEM, VMEM, HBM, HBM, HBM],
        HBM,
        [*vmem, pltpu.SemaphoreType.DMA((3 + planes,))],
        20,
    )(*lifted, control_t, east, north)
    return jnp.swapaxes(out.reshape(members, level_planes, lon, lat), 2, 3)


def solution(mesh):
    placed = (
        P("mem", "wide", None, None),
        P("mem", None, None, "wide", None),
        P("wide", None),
        P("wide", None),
        P(),
        P(),
        P(),
    )

    return jax.shard_map(
        local, mesh=mesh, in_specs=placed, out_specs=P("mem", "wide", None, None), check_vma=False
    )
```

time: 152 us -> 130 us (0.86)
  blocking collectives: 45.4 us -> 23.3 us
  local copies, waits for them, and re-layouts: 15.5 us -> 1.01 us
  Pallas kernels: 32.3 us -> 42 us
  starting transfers between devices: 10.9 us -> 20.6 us
  waiting for transfers between devices: 45.8 us -> 42.3 us
    all_to_all x2 -> x1, blocking collectives: 45.4 us -> 23.3 us  [exchange(): lax.all_to_all(sent.reshape(devices, -1, height, LANES), 'wide', 0, 0, ti...]
    unnamed x38 -> x10, local copies, waits for them, and re-layouts: 15.5 us -> 1.01 us
    pallas_call x8 -> x15, Pallas kernels: 32.3 us -> 42 us  [run(): pl.pallas_call(kernel, out_shape=out_shape, in_specs=ins or [VMEM] * len(...]
    all_to_all x2, starting transfers between devices: 8.48 us -> 16.2 us  [exchange(): lax.all_to_all(sent.reshape(devices, -1, height, LANES), 'wide', 0, 0, ti...]
    all_to_all x2, waiting for transfers between devices: 15.7 us -> 20.5 us  [exchange(): lax.all_to_all(sent.reshape(devices, -1, height, LANES), 'wide', 0, 0, ti...]
    ppermute x4 -> x6, waiting for transfers between devices: 26.2 us -> 21.8 us  [the longest x3 20 us: local(): got = lax.ppermute(on_chip, 'mem', next_chip)]
    ppermute x2 -> x3, waiting for transfers between devices: 3.98 us -> 0.01 us  [local(): other = lax.ppermute(own, 'mem', other_core)]
    ppermute x4 -> x6, starting transfers between devices: 2.27 us -> 4.01 us  [the longest x3 3.28 us: local(): got = lax.ppermute(on_chip, 'mem', next_chip)]
  transfers between devices with their start and end apart: 8 -> 11, of which waited for: 6 -> 5; matrix products, arithmetic and copies ran while one was open for 1% -> 0% of each run, Pallas kernels for 5% -> 12%
where the time goes in v3:
time: 130 us
  waiting for transfers between devices  42.3 us (33%)
  Pallas kernels  42 us (32%)
  blocking collectives  23.3 us (18%)
  starting transfers between devices  20.6 us (16%)
    pallas_call x15, Pallas kernels, run(): pl.pallas_call(kernel, out_shape=out_shape, in_specs=ins or [VMEM] * len(...  42 us
    all_to_all x1, blocking collectives, exchange(): lax.all_to_all(sent.reshape(devices, -1, height, LANES), 'wide', 0, 0, ti...  23.3 us
    all_to_all x2, waiting for transfers between devices, exchange(): lax.all_to_all(sent.reshape(devices, -1, height, LANES), 'wide', 0, 0, ti...  20.5 us
    ppermute x3, waiting for transfers between devices, local(): got = lax.ppermute(on_chip, 'mem', next_chip)  20 us
    all_to_all x2, starting transfers between devices, exchange(): lax.all_to_all(sent.reshape(devices, -1, height, LANES), 'wide', 0, 0, ti...  16.2 us
    ppermute x3, starting transfers between devices, local(): got = lax.ppermute(on_chip, 'mem', next_chip)  3.28 us
  transfers between devices with their start and end apart: 11, of which 5 were waited for; matrix products, arithmetic and copies ran while one was open for 0% of the time, Pallas kernels for 12%

profile of v3, /device:TPU:0, one launch (start us, length us, event | category | flops | bytes accessed | tf_op | source)
XLA Modules:
  0.0 129.6 jit_solution(12802478931834057713)
XLA Ops:
  0.0 0.0 copy-start
  0.0 1.0 copy-done
  1.0 12.0 %shard_map.74 = (f32[3072,128]{1,0:T(8,128)}, f32[4,90,8,128]{3,2,1,0:T(8,128)}, f32[4,90,8,128]{3,2,1,0:T(8,128)}) custom-call(f32[4,720,128]{2,1,0:T(8,128)} %bitcast.14, f32[720,128]{1,0:T(8,128)S(1)} %bitcast.13), custom_call_target="tpu_custom_call" | custom-call | flops 47185920 | bytes 2949120 | tf_op jit(solution)/shard_map/pallas_call | solution.py:301
  13.0 0.0 copy-start.1
  13.0 0.0 copy-start.2
  13.0 0.0 copy-start.3
  13.1 0.0 copy-start.4
  13.1 10.9 %all-to-all-start = ((f32[32,6,16,128]{3,2,1,0:T(8,128)}), f32[32,6,16,128]{3,2,1,0:T(8,128)S(1)}, u32[]{:S(2)}, u32[]{:S(2)}) async-start(f32[32,6,16,128]{3,2,1,0:T(8,128)} %bitcast.4), calls=%async_computation | async-start | bytes 3145728 | tf_op jit(solution)/shard_map/all_to_all | solution.py:362
  24.0 0.0 copy-done.1
  24.0 0.0 copy-done.2
  24.0 0.0 copy-done.3
  24.0 0.0 copy-done.4
  24.0 2.8 %shard_map.73 = (f32[256,256]{1,0:T(8,128)S(1)}, f32[256,256]{1,0:T(8,128)S(1)}, f32[384,256]{1,0:T(8,128)S(1)}, f32[384,256]{1,0:T(8,128)S(1)}, f32[384,256]{1,0:T(8,128)S(1)}) custom-call(s32[1]{0:T(128)} %bitcast.core_ref, f32[64,64]{1,0:T(8,128)S(1)} %copy-done.1, f32[8,192]{1,0:T(8,128)S(1)} %copy-done.4, s32[4,720]{1,0:T(4,128)S(1)} %copy-done.2, ...), custom_call_target="tpu_custom_call" | custom-call | flops 268435456 | bytes 4194304 | tf_op jit(solution)/shard_map/pallas_call | solution.py:301
  26.9 20.5 %all-to-all-done.pieces_ref = f32[32,6,16,128]{3,2,1,0:T(8,128)S(1)} async-done(((f32[32,6,16,128]{3,2,1,0:T(8,128)}), f32[32,6,16,128]{3,2,1,0:T(8,128)S(1)}, u32[]{:S(2)}, u32[]{:S(2)}) %all-to-all-start) | async-done | bytes 1572896 | tf_op jit(solution)/shard_map/all_to_all | solution.py:362
  47.4 2.2 %shard_map.75 = (f32[384,256]{1,0:T(8,128)S(1)}, f32[384,256]{1,0:T(8,128)S(1)}) custom-call(s32[1]{0:T(128)} %bitcast.core_ref, f32[256,256]{1,0:T(8,128)S(1)} %get-tuple-element.21.band_ref, f32[32,6,16,128]{3,2,1,0:T(8,128)S(1)} %all-to-all-done.pieces_ref, f32[2,3,64,4,720]{4,3,2,1,0:T(4,128)} %perturb_ref.11), custom_call_target="tpu_custom_call" | custom-call | flops 536870912 | bytes 5898240 | tf_op jit(solution)/shard_map/pallas_call | solution.py:301
  49.6 0.1 collective-permute-start
  49.7 1.7 %collective-permute-done.got_ref = f32[384,256]{1,0:T(8,128)S(1)} collective-permute-done((f32[384,256]{1,0:T(8,128)S(1)}, f32[384,256]{1,0:T(8,128)S(1)}, u32[]{:S(2)}, u32[]{:S(2)}) %collective-permute-start) | collective-permute-done | bytes 393248 | tf_op jit(solution)/shard_map/ppermute | solution.py:401
  51.4 1.1 collective-permute-start.1
  52.5 2.2 %shard_map.82 = (f32[384,256]{1,0:T(8,128)S(1)}, f32[384,256]{1,0:T(8,128)S(1)}) custom-call(s32[1]{0:T(128)} %bitcast.core_ref, f32[256,256]{1,0:T(8,128)S(1)} %get-tuple-element.21.band_ref, f32[32,6,16,128]{3,2,1,0:T(8,128)S(1)} %all-to-all-done.pieces_ref, f32[2,3,64,4,720]{4,3,2,1,0:T(4,128)} %perturb_ref.11), custom_call_target="tpu_custom_call" | custom-call | flops 536870912 | bytes 5898240 | tf_op jit(solution)/shard_map/pallas_call | solution.py:301
  54.7 0.1 collective-permute-start.6
  54.8 2.2 %shard_map.79 = (f32[384,256]{1,0:T(8,128)S(1)}, f32[384,256]{1,0:T(8,128)S(1)}) custom-call(s32[1]{0:T(128)} %bitcast.core_ref, f32[256,256]{1,0:T(8,128)S(1)} %get-tuple-element.21.band_ref, f32[32,6,16,128]{3,2,1,0:T(8,128)S(1)} %all-to-all-done.pieces_ref, f32[2,3,64,4,720]{4,3,2,1,0:T(4,128)} %perturb_ref.11), custom_call_target="tpu_custom_call" | custom-call | flops 536870912 | bytes 5898240 | tf_op jit(solution)/shard_map/pallas_call | solution.py:301
  57.1 0.6 collective-permute-start.3
  57.6 5.1 %collective-permute-done.1.got_ref = f32[384,256]{1,0:T(8,128)S(1)} collective-permute-done((f32[384,256]{1,0:T(8,128)S(1)}, f32[384,256]{1,0:T(8,128)S(1)}, u32[]{:S(2)}, u32[]{:S(2)}) %collective-permute-start.1) | collective-permute-done | bytes 393248 | tf_op jit(solution)/shard_map/ppermute | solution.py:403
  62.7 0.1 shard_map.77.own_ref
  62.7 0.1 collective-permute-start.2
  62.8 0.0 collective-permute-done.6.got_ref
  62.9 1.1 collective-permute-start.7
  64.0 0.0 collective-permute-done.3.got_ref
  64.0 1.1 collective-permute-start.4
  65.1 0.0 collective-permute-done.2.other_ref
  65.1 2.9 %shard_map.78 = f32[32,2,16,128]{3,2,1,0:T(8,128)} custom-call(s32[1]{0:T(128)} %bitcast.core_ref, f32[256,256]{1,0:T(8,128)S(1)} %get-tuple-element.19.band_ref, f32[384,256]{1,0:T(8,128)S(1)} %shard_map.77.own_ref, f32[384,256]{1,0:T(8,128)S(1)} %collective-permute-done.2.other_ref, f32[2,3,64,4,720]{4,3,2,1,0:T(4,128)} %perturb_ref.11), custom_call_target="tpu_custom_call" | custom-call | flops 536870912 | bytes 5898240 | tf_op jit(solution)/shard_map/pallas_call | solution.py:301
  68.0 5.3 %all-to-all-start.1 = ((f32[32,2,16,128]{3,2,1,0:T(8,128)}), f32[32,2,16,128]{3,2,1,0:T(8,128)S(1)}, u32[]{:S(2)}, u32[]{:S(2)}) async-start(f32[32,2,16,128]{3,2,1,0:T(8,128)} %shard_map.78), calls=%async_computation.1 | async-start | bytes 1048576 | tf_op jit(solution)/shard_map/all_to_all | solution.py:362
  73.3 1.7 %collective-permute-done.7.got_ref = f32[384,256]{1,0:T(8,128)S(1)} collective-permute-done((f32[384,256]{1,0:T(8,128)S(1)}, f32[384,256]{1,0:T(8,128)S(1)}, u32[]{:S(2)}, u32[]{:S(2)}) %collective-permute-start.7) | collective-permute-done | bytes 393248 | tf_op jit(solution)/shard_map/ppermute | solution.py:403
  75.0 0.1 shard_map.84.own_ref
  75.0 0.1 collective-permute-start.8
  75.1 13.3 %collective-permute-done.4.got_ref = f32[384,256]{1,0:T(8,128)} collective-permute-done((f32[384,256]{1,0:T(8,128)S(1)}, f32[384,256]{1,0:T(8,128)}, u32[]{:S(2)}, u32[]{:S(2)}) %collective-permute-start.4) | collective-permute-done | bytes 393248 | tf_op jit(solution)/shard_map/ppermute | solution.py:403
  88.4 1.1 shard_map.81.own_ref
  89.5 0.3 collective-permute-start.5
  89.8 0.0 collective-permute-done.8.other_ref
  89.8 2.2 %shard_map.85.rest_0_ = f32[32,4,16,128]{3,2,1,0:T(8,128)S(1)} custom-call(s32[1]{0:T(128)} %bitcast.core_ref, f32[256,256]{1,0:T(8,128)S(1)} %get-tuple-element.19.band_ref, f32[384,256]{1,0:T(8,128)S(1)} %shard_map.84.own_ref, f32[384,256]{1,0:T(8,128)S(1)} %collective-permute-done.8.other_ref, f32[2,3,64,4,720]{4,3,2,1,0:T(4,128)} %perturb_ref.11), custom_call_target="tpu_custom_call" | custom-call | flops 536870912 | bytes 5898240 | tf_op jit(solution)/shard_map/pallas_call | solution.py:301
  92.0 0.0 collective-permute-done.5.other_ref
  92.0 2.2 %shard_map.86 = f32[32,4,16,128]{3,2,1,0:T(8,128)S(1)} custom-call(s32[1]{0:T(128)} %bitcast.core_ref, f32[256,256]{1,0:T(8,128)S(1)} %get-tuple-element.19.band_ref, f32[384,256]{1,0:T(8,128)S(1)} %shard_map.81.own_ref, f32[384,256]{1,0:T(8,128)S(1)} %collective-permute-done.5.other_ref, ...), custom_call_target="tpu_custom_call", output_to_operand_aliasing={{}: (5, {})} | custom-call | flops 536870912 | bytes 5898240 | tf_op jit(solution)/shard_map/pallas_call | solution.py:301
  94.3 0.0 all-to-all-done.1
  94.3 23.3 %all_to_all.15 = f32[32,4,16,128]{3,2,1,0:T(8,128)S(1)} all-to-all(f32[32,4,16,128]{3,2,1,0:T(8,128)S(1)} %shard_map.86), channel_id=1, replica_groups=mesh['mem'=4,'wide'=32] {'wide'}, dimensions={0} | all-to-all | bytes 2097152 | tf_op jit(solution)/shard_map/all_to_all | solution.py:362
  117.6 11.8 %shard_map.87 = f32[4,720,128]{2,1,0:T(8,128)} custom-call(f32[1024,128]{1,0:T(8,128)S(1)} %bitcast.12, f32[2048,128]{1,0:T(8,128)S(1)} %bitcast.11, f32[4,720,128]{2,1,0:T(8,128)} %bitcast.15, f32[4,90,8,128]{3,2,1,0:T(8,128)} %get-tuple-element.31.east_hbm, f32[4,90,8,128]{3,2,1,0:T(8,128)} %get-tuple-element.32.north_hbm), custom_call_target="tpu_custom_call" | custom-call | flops 47185920 | bytes 4423680 | tf_op jit(solution)/shard_map/pallas_call | solution.py:301
  (3 shorter events, 0.1 us)
Async XLA Ops:
  0.0 1.0 copy-start
  13.0 11.0 %copy-start.1 = (f32[64,64]{1,0:T(8,128)S(1)}, f32[64,64]{1,0:T(8,128)}, u32[]{:S(2)}) copy-start(f32[64,64]{1,0:T(8,128)} %filter_ref.1) | copy-start | bytes 49156
  13.0 11.0 %copy-start.2 = (s32[4,720]{1,0:T(4,128)S(1)}, s32[4,720]{1,0:T(4,128)}, u32[]{:S(2)}) copy-start(s32[4,720]{1,0:T(4,128)} %count_ref.1) | copy-start | bytes 34564
  13.0 11.0 %copy-start.3 = (s32[4,720]{1,0:T(4,128)S(1)}, s32[4,720]{1,0:T(4,128)}, u32[]{:S(2)}) copy-start(s32[4,720]{1,0:T(4,128)} %kind_ref.1) | copy-start | bytes 34564
  13.1 11.0 %copy-start.4 = (f32[8,192]{1,0:T(8,128)S(1)}, f32[8,192]{1,0:T(8,128)}, u32[]{:S(2)}) copy-start(f32[8,192]{1,0:T(8,128)} %table_ref.1) | copy-start | bytes 18436
  13.1 34.3 %all-to-all-start = ((f32[32,6,16,128]{3,2,1,0:T(8,128)}), f32[32,6,16,128]{3,2,1,0:T(8,128)S(1)}, u32[]{:S(2)}, u32[]{:S(2)}) async-start(f32[32,6,16,128]{3,2,1,0:T(8,128)} %bitcast.4), calls=%async_computation | async-start | bytes 3145728 | tf_op jit(solution)/shard_map/all_to_all | solution.py:362
  49.6 1.8 %collective-permute-start = (f32[384,256]{1,0:T(8,128)S(1)}, f32[384,256]{1,0:T(8,128)S(1)}, u32[]{:S(2)}, u32[]{:S(2)}) collective-permute-start(f32[384,256]{1,0:T(8,128)S(1)} %get-tuple-element.24), channel_id=1, source_target_pairs={{0,32},{32,0},{64,96},{96,64},{1,33},{33,1},{65,97},{97,65},{2,34}... | collective-permute-start | bytes 1179656 | tf_op jit(solution)/shard_map/ppermute | solution.py:401
  51.4 11.2 %collective-permute-start.1 = (f32[384,256]{1,0:T(8,128)S(1)}, f32[384,256]{1,0:T(8,128)S(1)}, u32[]{:S(2)}, u32[]{:S(2)}) collective-permute-start(f32[384,256]{1,0:T(8,128)S(1)} %shard_map.76.on_chip_ref), channel_id=1, source_target_pairs={{0,64},{32,96},{64,0},{96,32},{1,65},{33,97},{65,1},{97,33},{2,66}... | collective-permute-start | bytes 1179656 | tf_op jit(solution)/shard_map/ppermute | solution.py:403
  54.7 8.1 %collective-permute-start.6 = (f32[384,256]{1,0:T(8,128)S(1)}, f32[384,256]{1,0:T(8,128)S(1)}, u32[]{:S(2)}, u32[]{:S(2)}) collective-permute-start(f32[384,256]{1,0:T(8,128)S(1)} %get-tuple-element.30), channel_id=1, source_target_pairs={{0,32},{32,0},{64,96},{96,64},{1,33},{33,1},{65,97},{97,65},{2,34}... | collective-permute-start | bytes 1179656 | tf_op jit(solution)/shard_map/ppermute | solution.py:401
  57.1 6.9 %collective-permute-start.3 = (f32[384,256]{1,0:T(8,128)S(1)}, f32[384,256]{1,0:T(8,128)S(1)}, u32[]{:S(2)}, u32[]{:S(2)}) collective-permute-start(f32[384,256]{1,0:T(8,128)S(1)} %get-tuple-element.27), channel_id=1, source_target_pairs={{0,32},{32,0},{64,96},{96,64},{1,33},{33,1},{65,97},{97,65},{2,34}... | collective-permute-start | bytes 1179656 | tf_op jit(solution)/shard_map/ppermute | solution.py:401
  62.7 2.4 %collective-permute-start.2 = (f32[384,256]{1,0:T(8,128)S(1)}, f32[384,256]{1,0:T(8,128)S(1)}, u32[]{:S(2)}, u32[]{:S(2)}) collective-permute-start(f32[384,256]{1,0:T(8,128)S(1)} %shard_map.77.own_ref), channel_id=1, source_target_pairs={{0,32},{32,0},{64,96},{96,64},{1,33},{33,1},{65,97},{97,65},{2,34}... | collective-permute-start | bytes 1179656 | tf_op jit(solution)/shard_map/ppermute | solution.py:405
  62.9 12.1 %collective-permute-start.7 = (f32[384,256]{1,0:T(8,128)S(1)}, f32[384,256]{1,0:T(8,128)S(1)}, u32[]{:S(2)}, u32[]{:S(2)}) collective-permute-start(f32[384,256]{1,0:T(8,128)S(1)} %shard_map.83.on_chip_ref), channel_id=1, source_target_pairs={{0,64},{32,96},{64,0},{96,32},{1,65},{33,97},{65,1},{97,33},{2,66}... | collective-permute-start | bytes 1179656 | tf_op jit(solution)/shard_map/ppermute | solution.py:403
  64.0 24.4 %collective-permute-start.4 = (f32[384,256]{1,0:T(8,128)S(1)}, f32[384,256]{1,0:T(8,128)}, u32[]{:S(2)}, u32[]{:S(2)}) collective-permute-start(f32[384,256]{1,0:T(8,128)S(1)} %shard_map.80.on_chip_ref), channel_id=1, source_target_pairs={{0,64},{32,96},{64,0},{96,32},{1,65},{33,97},{65,1},{97,33},{2,66}... | collective-permute-start | bytes 1179656 | tf_op jit(solution)/shard_map/ppermute | solution.py:403
  68.0 26.3 %all-to-all-start.1 = ((f32[32,2,16,128]{3,2,1,0:T(8,128)}), f32[32,2,16,128]{3,2,1,0:T(8,128)S(1)}, u32[]{:S(2)}, u32[]{:S(2)}) async-start(f32[32,2,16,128]{3,2,1,0:T(8,128)} %shard_map.78), calls=%async_computation.1 | async-start | bytes 1048576 | tf_op jit(solution)/shard_map/all_to_all | solution.py:362
  75.0 14.8 %collective-permute-start.8 = (f32[384,256]{1,0:T(8,128)S(1)}, f32[384,256]{1,0:T(8,128)S(1)}, u32[]{:S(2)}, u32[]{:S(2)}) collective-permute-start(f32[384,256]{1,0:T(8,128)S(1)} %shard_map.84.own_ref), channel_id=1, source_target_pairs={{0,32},{32,0},{64,96},{96,64},{1,33},{33,1},{65,97},{97,65},{2,34}... | collective-permute-start | bytes 1179656 | tf_op jit(solution)/shard_map/ppermute | solution.py:405
  89.5 2.5 %collective-permute-start.5 = (f32[384,256]{1,0:T(8,128)S(1)}, f32[384,256]{1,0:T(8,128)S(1)}, u32[]{:S(2)}, u32[]{:S(2)}) collective-permute-start(f32[384,256]{1,0:T(8,128)S(1)} %shard_map.81.own_ref), channel_id=1, source_target_pairs={{0,32},{32,0},{64,96},{96,64},{1,33},{33,1},{65,97},{97,65},{2,34}... | collective-permute-start | bytes 1179656 | tf_op jit(solution)/shard_map/ppermute | solution.py:405

commit v4 on v3

--- a/solution.py
+++ b/solution.py
@@ -93,20 +93,23 @@
 
 
 def spread_out(
-    control_hbm, diff_ref, sent_ref, east_hbm, north_hbm,
-    control, east, north, field, turned, flat, sems,
+    control_hbm, diff_hbm, sent_ref, east_hbm, north_hbm,
+    diffusivity, control, east, north, field, turned, flat, sems,
 ):
     planes, lon, lat = control.shape
     rows, steps = field.shape[:2]
     blocks = lat // rows
     tiles = turned.shape[0]
-    fetch = pltpu.make_async_copy(control_hbm, control, sems.at[0])
+    fetch_diff = pltpu.make_async_copy(diff_hbm, diffusivity, sems.at[0])
+    fetch_diff.start()
+    fetch = pltpu.make_async_copy(control_hbm, control, sems.at[1])
     fetch.start()
     turned[tiles - 1] = jnp.zeros(turned.shape[1:], jnp.float32)
     flat[:, (tiles - 1) * LANES :, :] = jnp.zeros((rows, LANES, LANES), jnp.float32)
-    coefficients(diff_ref, east, north, turned, flat)
-    keep_east = pltpu.make_async_copy(east, east_hbm, sems.at[1])
-    keep_north = pltpu.make_async_copy(north, north_hbm, sems.at[2])
+    fetch_diff.wait()
+    coefficients(diffusivity, east, north, turned, flat)
+    keep_east = pltpu.make_async_copy(east, east_hbm, sems.at[2])
+    keep_north = pltpu.make_async_copy(north, north_hbm, sems.at[3])
     keep_east.start()
     keep_north.start()
     fetch.wait()
@@ -149,7 +152,7 @@
     tiles_a = a_ref.shape[0] // (blocks * planes * rows)
     tiles_b = b_ref.shape[0] // (blocks * planes * rows)
     fetches = [
-        pltpu.make_async_copy(source, target, sems.at[n])
+        pltpu.make_async_copy(source, target, sems.at[planes + n])
         for n, (source, target) in enumerate(
             ((east_hbm, east), (north_hbm, north), (control_hbm, control))
         )
@@ -170,8 +173,8 @@
             flat[i, start : start + LANES, :] = jnp.concatenate(picked, 0).T
         for r in range(steps):
             field[i, r] = flat[i, pl.ds(r, SUB, stride=steps), :]
-    for fetch in fetches:
-        fetch.wait()
+    fetches[0].wait()
+    fetches[1].wait()
     diffuse_in_place(field, east, north)
     for i in range(rows):
         for r in range(steps):
@@ -182,13 +185,14 @@
                 turned[start // LANES, pl.ds(lat * q + i, blocks, stride=rows), :] = block[
                     q * blocks : (q + 1) * blocks, :
                 ]
+    fetches[2].wait()
     stores = []
     for q in range(planes):
         for start, width in blocks_of(lon):
             back = turned[start // LANES, lat * q : lat * q + lat, :].T
             place = pl.ds(start, width)
             control[q, place, :] = control[q, place, :] + back[:width, :]
-        stores.append(pltpu.make_async_copy(control.at[q], out_hbm.at[q], sems.at[3 + q]))
+        stores.append(pltpu.make_async_copy(control.at[q], out_hbm.at[q], sems.at[q]))
         stores[-1].start()
     for store in stores:
         store.wait()
@@ -200,7 +204,7 @@
     rows = flat // levels
     kinds, columns = table_ref.shape
     lon = count_ref.shape[1]
-    own, width = weight_refs[0].shape
+    own = weight_refs[0].shape[0]
     variables = columns // levels
     share = own // variables // rows
     spread = ones_where(iota((flat, levels), 0) // rows == iota((flat, levels), 1))
@@ -225,61 +229,86 @@
     count = dot(repeat, count_ref[...].astype(jnp.float32))
     which = (iota((wide, lon), 0) // rows).astype(jnp.float32)
     chosen = jnp.where(kind == which, count, 0.0)
-    for h, weight_ref in enumerate(weight_refs):
-        used = min(width, lon - h * width)
-        if used < width:
-            weight_ref[:, used:] = jnp.zeros((own, width - used), jnp.float32)
-        weight_ref[:, :used] = dot(table, chosen[:, h * width : h * width + used])
-
-
-def level_pair(perturb_ref, k, v, level, rows):
-    return jnp.concatenate([perturb_ref[k, v, level + u] for u in range(SUB // rows)], 0)
-
-
-def partial_sums(core_ref, band_ref, pieces_ref, perturb_ref, send_ref, keep_ref, filtered):
-    members, variables, levels, rows = perturb_ref.shape[:4]
-    flat = levels * rows
+    start = 0
+    for weight_ref in weight_refs[:-1]:
+        width = weight_ref.shape[1]
+        weight_ref[...] = dot(table, chosen[:, start : start + width])
+        start += width
+    tail = jnp.concatenate(
+        [chosen[:, start:], jnp.zeros((wide, start + LANES - lon), jnp.float32)], 1
+    )
+    weight_refs[-1][...] = dot(table, tail).T[: lon - start, :]
+
+
+def rows_of(perturb_ref, out_ref):
+    levels, rows, lon = perturb_ref.shape
+    pair = SUB // rows
+    for tile, (start, width) in enumerate(blocks_of(lon)):
+        if width < LANES:
+            out_ref[tile] = jnp.zeros(out_ref.shape[1:], jnp.float32)
+        for t in range(levels // pair):
+            out_ref[tile, SUB * t : SUB * t + SUB, :width] = jnp.concatenate(
+                [perturb_ref[pair * t + u, :, start : start + width] for u in range(pair)], 0
+            )
+
+
+def partial_sums(core_ref, band_ref, pieces_ref, perturb_ref, send_ref, keep_ref, filtered, parts):
+    members, flat = filtered.shape[1] // LANES, perturb_ref.shape[1]
+    variables = perturb_ref.shape[0] // members
     piece = pieces_ref.shape[1] // members
+    core = core_ref[0]
+    half = flat // 2
     mine = [
         pieces_ref[:, piece * k : piece * k + piece, :].reshape(flat, LANES)
         for k in range(members)
     ]
     filtered[...] = dot(band_ref[...], jnp.concatenate(mine, 1))
-    core = core_ref[0]
-    half = flat // 2
     for side, out_ref in enumerate((send_ref, keep_ref)):
-        part = core if side else 1 - core
+        base = (core if side else 1 - core) * half
+        turned = out_ref.shape[0] < variables * half
+        to_ref = parts.at[side] if turned else out_ref
         for t in range(half // SUB):
-            at = pl.ds(pl.multiple_of(part * half + t * SUB, SUB), SUB)
-            level = part * (levels // 2) + t * (SUB // rows)
+            at = pl.ds(pl.multiple_of(base + t * SUB, SUB), SUB)
             fields = [filtered[at, LANES * k : LANES * (k + 1)] for k in range(members)]
             for v in range(variables):
-                total = level_pair(perturb_ref, 0, v, level, rows) * fields[0]
+                total = perturb_ref[v, at, :] * fields[0]
                 for k in range(1, members):
-                    total = total + level_pair(perturb_ref, k, v, level, rows) * fields[k]
-                out_ref[v * half + t * SUB : v * half + t * SUB + SUB, :] = total
+                    total = total + perturb_ref[k * variables + v, at, :] * fields[k]
+                row = v * half + t * SUB
+                to_ref[row : row + SUB, :] = total
+        if turned:
+            for v in range(variables):
+                block = parts[side, v * half : (v + 1) * half, :].T
+                out_ref[:, v * half : (v + 1) * half] = block[: out_ref.shape[0], :]
 
 
 def lift(core_ref, band_ref, own_ref, other_ref, perturb_ref, *rest):
-    out_ref, adjoint = rest[-2:]
-    members, variables, levels, rows = perturb_ref.shape[:4]
-    flat = levels * rows
+    out_ref, adjoint, parts = rest[-3:]
+    members, flat = adjoint.shape[1] // LANES, perturb_ref.shape[1]
+    variables = perturb_ref.shape[0] // members
     piece = out_ref.shape[1] // members
     core = core_ref[0]
     half = flat // 2
-    for side, weighted in enumerate((own_ref, other_ref)):
-        part = core if side == 0 else 1 - core
+    sides = [own_ref, other_ref]
+    if own_ref.shape[0] < variables * half:
+        empty = jnp.zeros((LANES - own_ref.shape[0], half), jnp.float32)
+        for side, weighted in enumerate(sides):
+            for v in range(variables):
+                block = jnp.concatenate([weighted[:, v * half : (v + 1) * half], empty], 0)
+                parts[side, v * half : (v + 1) * half, :] = block.T
+        sides = [parts.at[0], parts.at[1]]
+    for side, weighted in enumerate(sides):
+        base = (core if side == 0 else 1 - core) * half
         for t in range(half // SUB):
-            at = pl.ds(pl.multiple_of(part * half + t * SUB, SUB), SUB)
-            level = part * (levels // 2) + t * (SUB // rows)
-            parts = [
+            at = pl.ds(pl.multiple_of(base + t * SUB, SUB), SUB)
+            terms = [
                 weighted[v * half + t * SUB : v * half + t * SUB + SUB, :]
                 for v in range(variables)
             ]
             for k in range(members):
-                total = level_pair(perturb_ref, k, 0, level, rows) * parts[0]
+                total = perturb_ref[k * variables, at, :] * terms[0]
                 for v in range(1, variables):
-                    total = total + level_pair(perturb_ref, k, v, level, rows) * parts[v]
+                    total = total + perturb_ref[k * variables + v, at, :] * terms[v]
                 adjoint[at, LANES * k : LANES * (k + 1)] = total
     whole = dot(band_ref[...], adjoint[...])
     for k in range(members):
@@ -324,9 +353,9 @@
     steps = lon // SUB
     flat = levels * rows
     half = flat // 2
-    chunk = 2
-    tiles = -(-lon // (chunk * LANES)) * chunk
-    width = chunk * LANES
+    tiles = -(-lon // LANES)
+    chunks = [(0, 1), (1, 1), (2, tiles - 3), (tiles - 1, 1)]
+    groups = {0: (0, 2), 1: (0, 2), 2: (2, tiles - 2), 3: (2, tiles - 2)}
     height = planes * rows
     control_t = jnp.swapaxes(control, 2, 3).reshape(planes, lon, lat)
     control_t = pltpu.with_memory_space_constraint(control_t, pltpu.HBM)
@@ -343,19 +372,20 @@
         (rows, tiles * LANES, LANES),
     ]
     vmem = [pltpu.VMEM(shape, jnp.float32) for shape in vmem]
+    resting = pltpu.HBM(coefs.shape, jnp.float32)
     work = planes * lat * lon * ITERS * 8
     size = planes * lat * lon * 4
 
     sent, east, north = call(
         spread_out,
-        [f32(devices * tiles * height, LANES)] + [pltpu.HBM(coefs.shape, coefs.dtype)] * 2,
+        [f32(devices * tiles * height, LANES), resting, resting],
         work,
         2 * size,
-        [HBM, VMEM],
+        [HBM, HBM],
         [VMEM, HBM, HBM],
-        [*vmem, pltpu.SemaphoreType.DMA((3,))],
+        [pltpu.VMEM((lon, lat), jnp.float32), *vmem, pltpu.SemaphoreType.DMA((4,))],
         20,
-    )(control_t, diff_t)
+    )(control_t, pltpu.with_memory_space_constraint(diff_t, pltpu.HBM))
     east, north = (pltpu.with_memory_space_constraint(e, pltpu.HBM) for e in (east, north))
 
     def exchange(sent):
@@ -363,64 +393,80 @@
 
     pieces = exchange(sent)
 
-    part = f32(variables * half, width)
+    used = lon - (tiles - 1) * LANES
+    parts = [f32(variables * half, count * LANES) for first, count in chunks[:-1]]
+    parts.append(f32(used, variables * half))
     band, band_t, *weights = call(
         prepare,
-        [f32(flat, flat), f32(flat, flat)] + [part] * (tiles // chunk),
+        [f32(flat, flat), f32(flat, flat)] + parts,
         1 << 28,
         4 << 20,
         [SMEM] + [VMEM] * 4,
     )(core, band_filter, obs_table, obs_count, obs_kind)
+    perturb = perturb.reshape(members * variables, levels, rows, lon)
+    perturb = call(
+        rows_of,
+        f32(tiles, members * variables, flat, LANES),
+        1 << 20,
+        6 * size,
+        [pl.BlockSpec((None, levels, rows, lon), lambda g: (g, 0, 0, 0))],
+        pl.BlockSpec((tiles, None, flat, LANES), lambda g: (0, g, 0, 0)),
+        grid=(members * variables,),
+    )(pltpu.with_memory_space_constraint(perturb, pltpu.HBM))
+    perturb = pltpu.with_memory_space_constraint(perturb, pltpu.HBM)
 
     other_core = [(i, i ^ 1) for i in range(4)]
     next_chip = [(i, i ^ 2) for i in range(4)]
-    perturb = pltpu.with_memory_space_constraint(perturb, pltpu.HBM)
-    in_band = pl.BlockSpec((flat, flat), lambda g: (0, 0))
-    in_part = pl.BlockSpec((variables * half, LANES), lambda g: (0, g))
-    scratch = [pltpu.VMEM((flat, members * LANES), jnp.float32)]
     home = None
     lifted = []
-    for h in range(tiles // chunk):
-        in_piece = pl.BlockSpec(
-            (devices, None, height, LANES), lambda g, h=h: (0, h * chunk + g, 0, 0)
+    for h, (first, count) in enumerate(chunks):
+        part = parts[h]
+        scratch = [
+            pltpu.VMEM((flat, members * LANES), jnp.float32),
+            pltpu.VMEM((2, variables * half, LANES), jnp.float32),
+        ]
+        in_band = pl.BlockSpec((flat, flat), lambda g: (0, 0))
+        in_part = pl.BlockSpec((part.shape[0], part.shape[1] // count), lambda g: (0, g))
+        in_perturb = pl.BlockSpec(
+            (None, members * variables, flat, LANES), lambda g, first=first: (first + g, 0, 0, 0)
         )
-        in_perturb = pl.BlockSpec(
-            (members, variables, levels, rows, LANES),
-            lambda g, h=h: (0, 0, 0, 0, h * chunk + g),
-        )
+
+        def piece_at(first):
+            return pl.BlockSpec(
+                (devices, None, height, LANES), lambda g, first=first: (0, first + g, 0, 0)
+            )
+
         send, keep = call(
             partial_sums,
             [part, part],
-            1 << 29,
-            4 * size,
-            [SMEM, in_band, in_piece, in_perturb],
+            count << 28,
+            count * size,
+            [SMEM, in_band, piece_at(first), in_perturb],
             [in_part, in_part],
             scratch,
-            grid=(chunk,),
+            grid=(count,),
         )(core, band, pieces, perturb)
         got = lax.ppermute(send, "mem", other_core)
         on_chip = call(add_up, part, 1 << 18, size)(keep, got)
         got = lax.ppermute(on_chip, "mem", next_chip)
         own = call(weigh, part, 1 << 18, size)(weights[h], on_chip, got)
         other = lax.ppermute(own, "mem", other_core)
-        first, last = h < 2, h != 1
-        count = chunk if h == 0 else tiles - chunk
-        out_piece = pl.BlockSpec(
-            (devices, None, height, LANES), lambda g, h=h: (0, max(h - 1, 0) * chunk + g, 0, 0)
-        )
+        start, total = groups[h]
+        begins = first == start
+
         home = call(
             lift,
-            f32(devices, count, height, LANES),
-            1 << 29,
-            4 * size,
+            f32(devices, total, height, LANES),
+            count << 28,
+            count * size,
             [SMEM, in_band, in_part, in_part, in_perturb]
-            + ([] if first else [pl.BlockSpec(memory_space=pl.ANY)]),
-            out_piece,
+            + ([] if begins else [pl.BlockSpec(memory_space=pl.ANY)]),
+            piece_at(first - start),
             scratch,
-            grid=(chunk,),
-            input_output_aliases={} if first else {5: 0},
-        )(core, band_t, own, other, perturb, *([] if first else [home]))
-        if last:
+            grid=(count,),
+            input_output_aliases={} if begins else {5: 0},
+        )(core, band_t, own, other, perturb, *([] if begins else [home]))
+        if first + count == start + total:
             lifted.append(exchange(home).reshape(-1, LANES))
 
     out = call(
@@ -430,7 +476,7 @@
         3 * size,
         [VMEM, VMEM, HBM, HBM, HBM],
         HBM,
-        [*vmem, pltpu.SemaphoreType.DMA((3 + planes,))],
+        [*vmem, pltpu.SemaphoreType.DMA((planes + 3,))],
         20,
     )(*lifted, control_t, east, north)
     return jnp.swapaxes(out.reshape(members, level_planes, lon, lat), 2, 3)

time: 130 us -> 143 us (1.10)
  Pallas kernels: 42 us -> 49.2 us
  blocking collectives: 23.3 us -> 26.4 us
  starting transfers between devices: 20.6 us -> 22.3 us
    pallas_call x15 -> x20, Pallas kernels: 42 us -> 49.2 us  [run(): pl.pallas_call(kernel, out_shape=out_shape, in_specs=ins or [VMEM] * len(...]
    all_to_all x2, waiting for transfers between devices: 20.5 us -> 14.1 us  [exchange(): lax.all_to_all(sent.reshape(devices, -1, height, LANES), 'wide', 0, 0, ti...]
    ppermute x3 -> x4, waiting for transfers between devices: 20 us -> 24 us  [local(): got = lax.ppermute(on_chip, 'mem', next_chip)]
    all_to_all x1, blocking collectives: 23.3 us -> 26.4 us  [exchange(): lax.all_to_all(sent.reshape(devices, -1, height, LANES), 'wide', 0, 0, ti...]
    ppermute x3 -> x4, waiting for transfers between devices: 1.71 us -> 3.32 us  [local(): got = lax.ppermute(send, 'mem', other_core)]
    ppermute x3 -> x4, starting transfers between devices: 3.28 us -> 4.38 us  [local(): got = lax.ppermute(on_chip, 'mem', next_chip)]
  transfers between devices with their start and end apart: 11 -> 14, of which waited for: 5 -> 6; matrix products, arithmetic and copies ran while one was open for 0% -> 0% of each run, Pallas kernels for 12% -> 15%
where the time goes in v4:
time: 143 us; the launch traced here: 142 us
  Pallas kernels  49.2 us (34%)
  waiting for transfers between devices  41.4 us (29%)
  blocking collectives  26.4 us (18%)
  starting transfers between devices  22.3 us (16%)
  local copies, waits for them, and re-layouts  2.16 us (2%)
    pallas_call x20, Pallas kernels, run(): pl.pallas_call(kernel, out_shape=out_shape, in_specs=ins or [VMEM] * len(...  49.2 us
    all_to_all x1, blocking collectives, exchange(): lax.all_to_all(sent.reshape(devices, -1, height, LANES), 'wide', 0, 0, ti...  26.4 us
    ppermute x4, waiting for transfers between devices, local(): got = lax.ppermute(on_chip, 'mem', next_chip)  24 us
    all_to_all x2, starting transfers between devices, exchange(): lax.all_to_all(sent.reshape(devices, -1, height, LANES), 'wide', 0, 0, ti...  16 us
    all_to_all x2, waiting for transfers between devices, exchange(): lax.all_to_all(sent.reshape(devices, -1, height, LANES), 'wide', 0, 0, ti...  14.1 us
    ppermute x4, starting transfers between devices, local(): got = lax.ppermute(on_chip, 'mem', next_chip)  4.38 us
    ppermute x4, waiting for transfers between devices, local(): got = lax.ppermute(send, 'mem', other_core)  3.32 us
  transfers between devices with their start and end apart: 14, of which 6 were waited for; matrix products, arithmetic and copies ran while one was open for 0% of the time, Pallas kernels for 15%

profile of v4, /device:TPU:0, one launch (start us, length us, event | category | flops | bytes accessed | tf_op | source)
XLA Modules:
  0.0 141.9 jit_solution(1333525477497168785)
XLA Ops:
  0.0 12.4 %shard_map.74 = (f32[3072,128]{1,0:T(8,128)}, f32[4,90,8,128]{3,2,1,0:T(8,128)}, f32[4,90,8,128]{3,2,1,0:T(8,128)}) custom-call(f32[4,720,128]{2,1,0:T(8,128)} %bitcast.14, f32[720,128]{1,0:T(8,128)} %bitcast.17), custom_call_target="tpu_custom_call" | custom-call | flops 47185920 | bytes 2949120 | tf_op jit(solution)/shard_map/pallas_call | solution.py:330
  12.5 10.8 %all-to-all-start = ((f32[32,6,16,128]{3,2,1,0:T(8,128)}), f32[32,6,16,128]{3,2,1,0:T(8,128)S(1)}, u32[]{:S(2)}, u32[]{:S(2)}) async-start(f32[32,6,16,128]{3,2,1,0:T(8,128)} %bitcast.4), calls=%async_computation | async-start | bytes 3145728 | tf_op jit(solution)/shard_map/all_to_all | solution.py:392
  23.2 0.0 copy-start.1
  23.2 0.0 copy-start.2
  23.3 0.0 copy-start.3
  23.3 0.0 copy-start.4
  23.3 4.3 %shard_map.75.perturb_ref = f32[6,6,256,128]{3,2,1,0:T(8,128)S(1)} custom-call(f32[6,64,4,720]{3,2,1,0:T(4,128)} %bitcast.16), custom_call_target="tpu_custom_call" | custom-call | flops 1048576 | bytes 8847360 | tf_op jit(solution)/shard_map/pallas_call | solution.py:330
  27.5 0.0 copy-start
  27.5 2.1 %copy-done = f32[6,6,256,128]{3,2,1,0:T(8,128)} copy-done((f32[6,6,256,128]{3,2,1,0:T(8,128)}, f32[6,6,256,128]{3,2,1,0:T(8,128)S(1)}, u32[]{:S(2)}) %copy-start) | copy-done | bytes 4718616
  29.7 0.0 copy-done.1
  29.7 0.0 copy-done.2
  29.7 0.0 copy-done.3
  29.7 0.0 copy-done.4
  29.7 2.9 %shard_map.73 = (f32[256,256]{1,0:T(8,128)S(1)}, f32[256,256]{1,0:T(8,128)S(1)}, f32[384,128]{1,0:T(8,128)S(1)}, f32[384,128]{1,0:T(8,128)S(1)}, f32[384,384]{1,0:T(8,128)S(1)}, /*index=5*/f32[80,384]{1,0:T(8,128)S(1)}) custom-call(s32[1]{0:T(128)} %bitcast.core_ref, f32[64,64]{1,0:T(8,128)S(1)} %copy-done.1, f32[8,192]{1,0:T(8,128)S(1)} %copy-done.4, ...), custom_call_target="tpu_custom_call" | custom-call | flops 268435456 | bytes 4194304 | tf_op jit(solution)/shard_map/pallas_call | solution.py:330
  32.6 14.1 %all-to-all-done.pieces_ref = f32[32,6,16,128]{3,2,1,0:T(8,128)S(1)} async-done(((f32[32,6,16,128]{3,2,1,0:T(8,128)}), f32[32,6,16,128]{3,2,1,0:T(8,128)S(1)}, u32[]{:S(2)}, u32[]{:S(2)}) %all-to-all-start) | async-done | bytes 1572896 | tf_op jit(solution)/shard_map/all_to_all | solution.py:392
  46.6 3.3 %shard_map.87 = (f32[384,384]{1,0:T(8,128)S(1)}, f32[384,384]{1,0:T(8,128)S(1)}) custom-call(s32[1]{0:T(128)} %bitcast.core_ref, f32[256,256]{1,0:T(8,128)S(1)} %get-tuple-element.24.band_ref, f32[32,6,16,128]{3,2,1,0:T(8,128)S(1)} %all-to-all-done.pieces_ref, f32[6,6,256,128]{3,2,1,0:T(8,128)} %copy-done), custom_call_target="tpu_custom_call" | custom-call | flops 805306368 | bytes 4423680 | tf_op jit(solution)/shard_map/pallas_call | solution.py:330
  49.9 0.1 collective-permute-start.9
  50.0 2.0 %collective-permute-done.9.got_ref = f32[384,384]{1,0:T(8,128)S(1)} collective-permute-done((f32[384,384]{1,0:T(8,128)S(1)}, f32[384,384]{1,0:T(8,128)S(1)}, u32[]{:S(2)}, u32[]{:S(2)}) %collective-permute-start.9) | collective-permute-done | bytes 589856 | tf_op jit(solution)/shard_map/ppermute | solution.py:449
  52.0 0.1 shard_map.88.on_chip_ref
  52.1 1.1 collective-permute-start.10
  53.2 1.6 %shard_map.79 = (f32[384,128]{1,0:T(8,128)S(1)}, f32[384,128]{1,0:T(8,128)S(1)}) custom-call(s32[1]{0:T(128)} %bitcast.core_ref, f32[256,256]{1,0:T(8,128)S(1)} %get-tuple-element.24.band_ref, f32[32,6,16,128]{3,2,1,0:T(8,128)S(1)} %all-to-all-done.pieces_ref, f32[6,6,256,128]{3,2,1,0:T(8,128)} %copy-done), custom_call_target="tpu_custom_call" | custom-call | flops 268435456 | bytes 1474560 | tf_op jit(solution)/shard_map/pallas_call | solution.py:330
  54.7 0.1 collective-permute-start.3
  54.8 1.6 %shard_map.76 = (f32[384,128]{1,0:T(8,128)S(1)}, f32[384,128]{1,0:T(8,128)S(1)}) custom-call(s32[1]{0:T(128)} %bitcast.core_ref, f32[256,256]{1,0:T(8,128)S(1)} %get-tuple-element.24.band_ref, f32[32,6,16,128]{3,2,1,0:T(8,128)S(1)} %all-to-all-done.pieces_ref, f32[6,6,256,128]{3,2,1,0:T(8,128)} %copy-done), custom_call_target="tpu_custom_call" | custom-call | flops 268435456 | bytes 1474560 | tf_op jit(solution)/shard_map/pallas_call | solution.py:330
  56.4 0.6 collective-permute-start
  57.0 0.0 collective-permute-done.3.got_ref
  57.0 1.1 collective-permute-start.4
  58.1 0.0 collective-permute-done.got_ref
  58.1 1.1 collective-permute-start.1
  59.2 13.3 %collective-permute-done.4.got_ref = f32[384,128]{1,0:T(8,128)S(1)} collective-permute-done((f32[384,128]{1,0:T(8,128)S(1)}, f32[384,128]{1,0:T(8,128)S(1)}, u32[]{:S(2)}, u32[]{:S(2)}) %collective-permute-start.4) | collective-permute-done | bytes 196640 | tf_op jit(solution)/shard_map/ppermute | solution.py:451
  72.6 0.1 collective-permute-start.5
  72.7 3.3 %collective-permute-done.1.got_ref = f32[384,128]{1,0:T(8,128)S(1)} collective-permute-done((f32[384,128]{1,0:T(8,128)S(1)}, f32[384,128]{1,0:T(8,128)S(1)}, u32[]{:S(2)}, u32[]{:S(2)}) %collective-permute-start.1) | collective-permute-done | bytes 196640 | tf_op jit(solution)/shard_map/ppermute | solution.py:451
  76.0 0.1 collective-permute-start.2
  76.1 0.0 collective-permute-done.10.got_ref
  76.1 0.1 shard_map.89.own_ref
  76.2 0.6 collective-permute-start.11
  76.8 0.0 collective-permute-done.5.other_ref
  76.8 2.3 %shard_map.82.rest_0_ = f32[32,2,16,128]{3,2,1,0:T(8,128)} custom-call(s32[1]{0:T(128)} %bitcast.core_ref, f32[256,256]{1,0:T(8,128)S(1)} %get-tuple-element.22.band_ref, f32[384,128]{1,0:T(8,128)S(1)} %shard_map.81.own_ref, f32[384,128]{1,0:T(8,128)S(1)} %collective-permute-done.5.other_ref, f32[6,6,256,128]{3,2,1,0:T(8,128)} %copy-done), custom_call_target="tpu_custom_call" | custom-call | flops 268435456 | bytes 1474560 | tf_op jit(solution)/shard_map/pallas_call | solution.py:330
  79.1 0.0 collective-permute-done.2.other_ref
  79.1 2.3 %shard_map.83 = f32[32,2,16,128]{3,2,1,0:T(8,128)} custom-call(s32[1]{0:T(128)} %bitcast.core_ref, f32[256,256]{1,0:T(8,128)S(1)} %get-tuple-element.22.band_ref, f32[384,128]{1,0:T(8,128)S(1)} %shard_map.78.own_ref, f32[384,128]{1,0:T(8,128)S(1)} %collective-permute-done.2.other_ref, f32[6,6,256,128]{3,2,1,0:T(8,128)} %copy-done, ...), custom_call_target="tpu_custom_call", output_to_operand_aliasing={{}: (5, {})} | custom-call | flops 268435456 | bytes 1474560 | tf_op jit(solution)/shard_map/pallas_call | solution.py:330
  81.3 5.3 %all-to-all-start.1 = ((f32[32,2,16,128]{3,2,1,0:T(8,128)}), f32[32,2,16,128]{3,2,1,0:T(8,128)S(1)}, u32[]{:S(2)}, u32[]{:S(2)}) async-start(f32[32,2,16,128]{3,2,1,0:T(8,128)} %shard_map.83), calls=%async_computation.1 | async-start | bytes 1048576 | tf_op jit(solution)/shard_map/all_to_all | solution.py:392
  86.6 1.7 %shard_map.84 = (f32[80,384]{1,0:T(8,128)S(1)}, f32[80,384]{1,0:T(8,128)S(1)}) custom-call(s32[1]{0:T(128)} %bitcast.core_ref, f32[256,256]{1,0:T(8,128)S(1)} %get-tuple-element.24.band_ref, f32[32,6,16,128]{3,2,1,0:T(8,128)S(1)} %all-to-all-done.pieces_ref, f32[6,6,256,128]{3,2,1,0:T(8,128)} %copy-done), custom_call_target="tpu_custom_call" | custom-call | flops 268435456 | bytes 1474560 | tf_op jit(solution)/shard_map/pallas_call | solution.py:330
  88.3 0.3 collective-permute-start.6
  88.6 1.3 collective-permute-done.6.got_ref
  89.9 1.1 collective-permute-start.7
  91.0 7.5 %collective-permute-done.7.got_ref = f32[80,384]{1,0:T(8,128)S(1)} collective-permute-done((f32[80,384]{1,0:T(8,128)S(1)}, f32[80,384]{1,0:T(8,128)S(1)}, u32[]{:S(2)}, u32[]{:S(2)}) %collective-permute-start.7) | collective-permute-done | bytes 122912 | tf_op jit(solution)/shard_map/ppermute | solution.py:451
  98.5 0.1 collective-permute-start.8
  98.6 0.0 collective-permute-done.11.other_ref
  98.6 3.5 %shard_map.90.rest_0_ = f32[32,4,16,128]{3,2,1,0:T(8,128)S(1)} custom-call(s32[1]{0:T(128)} %bitcast.core_ref, f32[256,256]{1,0:T(8,128)S(1)} %get-tuple-element.22.band_ref, f32[384,384]{1,0:T(8,128)S(1)} %shard_map.89.own_ref, f32[384,384]{1,0:T(8,128)} %collective-permute-done.11.other_ref, f32[6,6,256,128]{3,2,1,0:T(8,128)} %copy-done), custom_call_target="tpu_custom_call" | custom-call | flops 805306368 | bytes 4423680 | tf_op jit(solution)/shard_map/pallas_call | solution.py:330
  102.1 0.0 collective-permute-done.8.other_ref
  102.1 1.7 %shard_map.91 = f32[32,4,16,128]{3,2,1,0:T(8,128)S(1)} custom-call(s32[1]{0:T(128)} %bitcast.core_ref, f32[256,256]{1,0:T(8,128)S(1)} %get-tuple-element.22.band_ref, f32[80,384]{1,0:T(8,128)S(1)} %shard_map.86.own_ref, f32[80,384]{1,0:T(8,128)S(1)} %collective-permute-done.8.other_ref, f32[6,6,256,128]{3,2,1,0:T(8,128)} %copy-done, ...), custom_call_target="tpu_custom_call", output_to_operand_aliasing={{}: (5, {})} | custom-call | flops 268435456 | bytes 1474560 | tf_op jit(solution)/shard_map/pallas_call | solution.py:330
  103.8 0.0 all-to-all-done.1
  103.8 26.4 %all_to_all.15 = f32[32,4,16,128]{3,2,1,0:T(8,128)S(1)} all-to-all(f32[32,4,16,128]{3,2,1,0:T(8,128)S(1)} %shard_map.91), channel_id=1, replica_groups=mesh['mem'=4,'wide'=32] {'wide'}, dimensions={0} | all-to-all | bytes 2097152 | tf_op jit(solution)/shard_map/all_to_all | solution.py:392
  130.3 11.5 %shard_map.92 = f32[4,720,128]{2,1,0:T(8,128)} custom-call(f32[1024,128]{1,0:T(8,128)S(1)} %bitcast.13, f32[2048,128]{1,0:T(8,128)S(1)} %bitcast.12, f32[4,720,128]{2,1,0:T(8,128)} %bitcast.15, f32[4,90,8,128]{3,2,1,0:T(8,128)} %get-tuple-element.37.east_hbm, f32[4,90,8,128]{3,2,1,0:T(8,128)} %get-tuple-element.38.north_hbm), custom_call_target="tpu_custom_call" | custom-call | flops 47185920 | bytes 4423680 | tf_op jit(solution)/shard_map/pallas_call | solution.py:330
  (6 shorter events, 0.1 us)
Async XLA Ops:
  12.5 34.2 %all-to-all-start = ((f32[32,6,16,128]{3,2,1,0:T(8,128)}), f32[32,6,16,128]{3,2,1,0:T(8,128)S(1)}, u32[]{:S(2)}, u32[]{:S(2)}) async-start(f32[32,6,16,128]{3,2,1,0:T(8,128)} %bitcast.4), calls=%async_computation | async-start | bytes 3145728 | tf_op jit(solution)/shard_map/all_to_all | solution.py:392
  23.2 6.5 %copy-start.1 = (f32[64,64]{1,0:T(8,128)S(1)}, f32[64,64]{1,0:T(8,128)}, u32[]{:S(2)}) copy-start(f32[64,64]{1,0:T(8,128)} %filter_ref.1) | copy-start | bytes 49156
  23.2 6.4 %copy-start.2 = (s32[4,720]{1,0:T(4,128)S(1)}, s32[4,720]{1,0:T(4,128)}, u32[]{:S(2)}) copy-start(s32[4,720]{1,0:T(4,128)} %count_ref.1) | copy-start | bytes 34564
  23.3 6.4 %copy-start.3 = (s32[4,720]{1,0:T(4,128)S(1)}, s32[4,720]{1,0:T(4,128)}, u32[]{:S(2)}) copy-start(s32[4,720]{1,0:T(4,128)} %kind_ref.1) | copy-start | bytes 34564
  23.3 6.4 %copy-start.4 = (f32[8,192]{1,0:T(8,128)S(1)}, f32[8,192]{1,0:T(8,128)}, u32[]{:S(2)}) copy-start(f32[8,192]{1,0:T(8,128)} %table_ref.1) | copy-start | bytes 18436
  27.5 2.1 %copy-start = (f32[6,6,256,128]{3,2,1,0:T(8,128)}, f32[6,6,256,128]{3,2,1,0:T(8,128)S(1)}, u32[]{:S(2)}) copy-start(f32[6,6,256,128]{3,2,1,0:T(8,128)S(1)} %shard_map.75.perturb_ref) | copy-start | bytes 14155780
  49.9 2.1 %collective-permute-start.9 = (f32[384,384]{1,0:T(8,128)S(1)}, f32[384,384]{1,0:T(8,128)S(1)}, u32[]{:S(2)}, u32[]{:S(2)}) collective-permute-start(f32[384,384]{1,0:T(8,128)S(1)} %get-tuple-element.36), channel_id=1, source_target_pairs={{0,32},{32,0},{64,96},{96,64},{1,33},{33,1},{65,97},{97,65},{2,34}... | collective-permute-start | bytes 1769480 | tf_op jit(solution)/shard_map/ppermute | solution.py:449
  52.1 24.0 %collective-permute-start.10 = (f32[384,384]{1,0:T(8,128)S(1)}, f32[384,384]{1,0:T(8,128)S(1)}, u32[]{:S(2)}, u32[]{:S(2)}) collective-permute-start(f32[384,384]{1,0:T(8,128)S(1)} %shard_map.88.on_chip_ref), channel_id=1, source_target_pairs={{0,64},{32,96},{64,0},{96,32},{1,65},{33,97},{65,1},{97,33},{2,66}... | collective-permute-start | bytes 1769480 | tf_op jit(solution)/shard_map/ppermute | solution.py:451
  54.7 2.3 %collective-permute-start.3 = (f32[384,128]{1,0:T(8,128)S(1)}, f32[384,128]{1,0:T(8,128)S(1)}, u32[]{:S(2)}, u32[]{:S(2)}) collective-permute-start(f32[384,128]{1,0:T(8,128)S(1)} %get-tuple-element.30), channel_id=1, source_target_pairs={{0,32},{32,0},{64,96},{96,64},{1,33},{33,1},{65,97},{97,65},{2,34}... | collective-permute-start | bytes 589832 | tf_op jit(solution)/shard_map/ppermute | solution.py:449
  56.4 1.7 %collective-permute-start = (f32[384,128]{1,0:T(8,128)S(1)}, f32[384,128]{1,0:T(8,128)S(1)}, u32[]{:S(2)}, u32[]{:S(2)}) collective-permute-start(f32[384,128]{1,0:T(8,128)S(1)} %get-tuple-element.27), channel_id=1, source_target_pairs={{0,32},{32,0},{64,96},{96,64},{1,33},{33,1},{65,97},{97,65},{2,34}... | collective-permute-start | bytes 589832 | tf_op jit(solution)/shard_map/ppermute | solution.py:449
  57.0 15.5 %collective-permute-start.4 = (f32[384,128]{1,0:T(8,128)S(1)}, f32[384,128]{1,0:T(8,128)S(1)}, u32[]{:S(2)}, u32[]{:S(2)}) collective-permute-start(f32[384,128]{1,0:T(8,128)S(1)} %shard_map.80.on_chip_ref), channel_id=1, source_target_pairs={{0,64},{32,96},{64,0},{96,32},{1,65},{33,97},{65,1},{97,33},{2,66}... | collective-permute-start | bytes 589832 | tf_op jit(solution)/shard_map/ppermute | solution.py:451
  58.1 17.8 %collective-permute-start.1 = (f32[384,128]{1,0:T(8,128)S(1)}, f32[384,128]{1,0:T(8,128)S(1)}, u32[]{:S(2)}, u32[]{:S(2)}) collective-permute-start(f32[384,128]{1,0:T(8,128)S(1)} %shard_map.77.on_chip_ref), channel_id=1, source_target_pairs={{0,64},{32,96},{64,0},{96,32},{1,65},{33,97},{65,1},{97,33},{2,66}... | collective-permute-start | bytes 589832 | tf_op jit(solution)/shard_map/ppermute | solution.py:451
  72.6 4.2 %collective-permute-start.5 = (f32[384,128]{1,0:T(8,128)S(1)}, f32[384,128]{1,0:T(8,128)S(1)}, u32[]{:S(2)}, u32[]{:S(2)}) collective-permute-start(f32[384,128]{1,0:T(8,128)S(1)} %shard_map.81.own_ref), channel_id=1, source_target_pairs={{0,32},{32,0},{64,96},{96,64},{1,33},{33,1},{65,97},{97,65},{2,34}... | collective-permute-start | bytes 589832 | tf_op jit(solution)/shard_map/ppermute | solution.py:453
  76.0 3.1 %collective-permute-start.2 = (f32[384,128]{1,0:T(8,128)S(1)}, f32[384,128]{1,0:T(8,128)S(1)}, u32[]{:S(2)}, u32[]{:S(2)}) collective-permute-start(f32[384,128]{1,0:T(8,128)S(1)} %shard_map.78.own_ref), channel_id=1, source_target_pairs={{0,32},{32,0},{64,96},{96,64},{1,33},{33,1},{65,97},{97,65},{2,34}... | collective-permute-start | bytes 589832 | tf_op jit(solution)/shard_map/ppermute | solution.py:453
  76.2 22.4 %collective-permute-start.11 = (f32[384,384]{1,0:T(8,128)S(1)}, f32[384,384]{1,0:T(8,128)}, u32[]{:S(2)}, u32[]{:S(2)}) collective-permute-start(f32[384,384]{1,0:T(8,128)S(1)} %shard_map.89.own_ref), channel_id=1, source_target_pairs={{0,32},{32,0},{64,96},{96,64},{1,33},{33,1},{65,97},{97,65},{2,34}... | collective-permute-start | bytes 1769480 | tf_op jit(solution)/shard_map/ppermute | solution.py:453
  81.3 22.5 %all-to-all-start.1 = ((f32[32,2,16,128]{3,2,1,0:T(8,128)}), f32[32,2,16,128]{3,2,1,0:T(8,128)S(1)}, u32[]{:S(2)}, u32[]{:S(2)}) async-start(f32[32,2,16,128]{3,2,1,0:T(8,128)} %shard_map.83), calls=%async_computation.1 | async-start | bytes 1048576 | tf_op jit(solution)/shard_map/all_to_all | solution.py:392
  88.3 1.6 %collective-permute-start.6 = (f32[80,384]{1,0:T(8,128)S(1)}, f32[80,384]{1,0:T(8,128)S(1)}, u32[]{:S(2)}, u32[]{:S(2)}) collective-permute-start(f32[80,384]{1,0:T(8,128)S(1)} %get-tuple-element.33), channel_id=1, source_target_pairs={{0,32},{32,0},{64,96},{96,64},{1,33},{33,1},{65,97},{97,65},{2,34}... | collective-permute-start | bytes 368648 | tf_op jit(solution)/shard_map/ppermute | solution.py:449
  89.9 8.6 %collective-permute-start.7 = (f32[80,384]{1,0:T(8,128)S(1)}, f32[80,384]{1,0:T(8,128)S(1)}, u32[]{:S(2)}, u32[]{:S(2)}) collective-permute-start(f32[80,384]{1,0:T(8,128)S(1)} %shard_map.85.on_chip_ref), channel_id=1, source_target_pairs={{0,64},{32,96},{64,0},{96,32},{1,65},{33,97},{65,1},{97,33},{2,66}... | collective-permute-start | bytes 368648 | tf_op jit(solution)/shard_map/ppermute | solution.py:451
  98.5 3.6 %collective-permute-start.8 = (f32[80,384]{1,0:T(8,128)S(1)}, f32[80,384]{1,0:T(8,128)S(1)}, u32[]{:S(2)}, u32[]{:S(2)}) collective-permute-start(f32[80,384]{1,0:T(8,128)S(1)} %shard_map.86.own_ref), channel_id=1, source_target_pairs={{0,32},{32,0},{64,96},{96,64},{1,33},{33,1},{65,97},{97,65},{2,34}... | collective-permute-start | bytes 368648 | tf_op jit(solution)/shard_map/ppermute | solution.py:453
